TPU v7x, 256 devices: a whole 4x4x8 slice. The times are simulated.
256 devices in a mesh: chain: 8 (over z), inner: 32 (over y, x, core).
Axes of the slice: x: 4, y: 4, z: 8, core: 2. Of those that a mesh axis runs over, the one named last changes fastest.
Arguments:
- queries: bfloat16 [32768, 4096], P(('chain', 'inner')), may hold values from -0.75 to 0.75
- key_rows: bfloat16 [32768, 4096], P(('chain', 'inner')), may hold values from -0.75 to 0.75
- value_rows: bfloat16 [32768, 4096], P(('chain', 'inner')), may hold values from -0.75 to 0.75
- out_grad: bfloat16 [32768, 4096], P(('chain', 'inner')), may hold values from -0.75 to 0.75
- log_decay: bfloat16 [32768, 32], P(('chain', 'inner')), may hold values from -2 to 0, as said below
Outputs:
- attended: bfloat16 [32768, 4096], P(('chain', 'inner'))
- query_grad: bfloat16 [32768, 4096], P(('chain', 'inner'))
- key_grad: bfloat16 [32768, 4096], P(('chain', 'inner'))
- value_grad: bfloat16 [32768, 4096], P(('chain', 'inner'))
Inputs may be any that keep to these rules, and one draw needn't show every extreme that they name: `log_decay`: every entry is negative.
All inputs are finite; a program needn't handle non-finite values.
Results may differ from a plain program's by a relative error of at most 0.0051.
Values may be sent and summed in bfloat16 or wider, within the bound.
No kernel may reach another device: no remote copies, remote signals or barrier semaphores. Data moves between devices by JAX's collectives and lax.ppermute only.
A program may use at most 64 MiB of HBM per device.

v0:
```python
import jax
import jax.numpy as jnp
from jax import lax
from jax.sharding import PartitionSpec as P

HEAD_SIZE = 128
BLOCK = 128


def carried_in(value, axis, join, neutral, backward):
    count, mine = (lax.axis_size(axis), lax.axis_index(axis))
    pieces = jax.tree.map(lambda part: lax.all_gather(part, axis), value)
    if backward:
        pieces = jax.tree.map(lambda part: part[::-1], pieces)
        mine = count - 1 - mine
    total = jax.tree.map(
        lambda part, zero: jnp.full_like(part, 0) + jnp.asarray(zero, part.dtype), value, neutral
    )

    def hop(position, total):
        longer = join(total, jax.tree.map(lambda part: part[position], pieces))
        return jax.tree.map(lambda new, old: jnp.where(position < mine, new, old), longer, total)

    return lax.fori_loop(0, count - 1, hop, total)


def combine(earlier, later):
    early_sum, early_state = earlier
    late_sum, late_state = later
    return (early_sum + late_sum, jnp.exp(late_sum)[..., None, None] * early_state + late_state)


def prefixes(sums, forward_terms, backward_terms):
    fwd_sum, fwd_state = lax.associative_scan(combine, (sums, forward_terms))
    rev_sum, rev_state = lax.associative_scan(combine, (sums, backward_terms), reverse=True)
    zero_sum = jnp.zeros_like(sums[:1])
    zero_state = jnp.zeros_like(forward_terms[:1])
    before_sum = jnp.concatenate([zero_sum, fwd_sum[:-1]], axis=0)
    before_state = jnp.concatenate([zero_state, fwd_state[:-1]], axis=0)
    after_sum = jnp.concatenate([rev_sum[1:], zero_sum], axis=0)
    after_state = jnp.concatenate([rev_state[1:], zero_state], axis=0)
    return (
        (before_sum, before_state, after_sum, after_state),
        (fwd_sum[-1], fwd_state[-1], rev_state[0]),
    )


def block_setup(decay_rows):
    rows, heads = decay_rows.shape
    blocks = rows // BLOCK
    decay_heads = decay_rows.astype(jnp.float32).T.reshape(heads, blocks, BLOCK).transpose(1, 0, 2)
    positions = jnp.arange(BLOCK)
    triangle = (positions[:, None] <= positions[None, :]).astype(jnp.float32)
    cumul = jnp.matmul(decay_heads, triangle, precision=lax.Precision.HIGHEST)
    return (cumul, cumul[..., -1])


def scale_pair(cumul, finals):
    forward_scale = jnp.exp(cumul).transpose(0, 2, 1)[..., None]
    backward_scale = jnp.exp(finals[..., None] - cumul).transpose(0, 2, 1)[..., None]
    return (forward_scale, backward_scale)


def local_states(query_blocks, key_blocks, value_blocks, grad_blocks, cumul, finals):
    forward_scale, backward_scale = scale_pair(cumul, finals)
    scaled_keys = (key_blocks * backward_scale).astype(jnp.bfloat16)
    scaled_queries = (query_blocks * forward_scale).astype(jnp.bfloat16)
    kv_terms = jnp.einsum(
        "jshd,jshe->jhde", scaled_keys, value_blocks, preferred_element_type=jnp.float32
    )
    qd_terms = jnp.einsum(
        "jthd,jthe->jhde", scaled_queries, grad_blocks, preferred_element_type=jnp.float32
    )
    return prefixes(finals, kv_terms, qd_terms)


def entries(parts, state_in, trail_in):
    before_sum, before_state, after_sum, after_state = parts
    entering = jnp.exp(before_sum)[..., None, None] * state_in[None] + before_state
    trailing = jnp.exp(after_sum)[..., None, None] * trail_in[None] + after_state
    return (entering, trailing)


def chain_states(total_sum, total_state, total_trail):
    zero_sum = jnp.zeros_like(total_sum)
    zero_state = jnp.zeros_like(total_state)
    moved_fwd = carried_in(
        (total_sum, total_state), "chain", combine, (zero_sum, zero_state), False
    )
    moved_rev = carried_in((total_sum, total_trail), "chain", combine, (zero_sum, zero_state), True)
    state_in = moved_fwd[1]
    trail_in = moved_rev[1]
    return (state_in, trail_in)


def block_results(
    query_blocks, key_blocks, value_blocks, grad_blocks, cumul, finals, entering, trailing
):
    enter_narrow = entering.astype(jnp.bfloat16)
    trail_narrow = trailing.astype(jnp.bfloat16)
    spread = cumul[..., :, None] - cumul[..., None, :]
    positions = jnp.arange(cumul.shape[2])
    lower = positions[:, None] >= positions[None, :]
    weights = jnp.exp(jnp.where(lower, spread, -jnp.inf))
    scores = jnp.einsum(
        "jthd,jshd->jhts", query_blocks, key_blocks, preferred_element_type=jnp.float32
    )
    probs = (scores * weights).astype(jnp.bfloat16)
    grow_scores = jnp.einsum(
        "jthe,jshe->jhts", grad_blocks, value_blocks, preferred_element_type=jnp.float32
    )
    grows = (grow_scores * weights).astype(jnp.bfloat16)
    forward_scale, backward_scale = scale_pair(cumul, finals)
    attended = jnp.einsum(
        "jhts,jshe->jthe", probs, value_blocks, preferred_element_type=jnp.float32
    ) + forward_scale * jnp.einsum(
        "jthd,jhde->jthe", query_blocks, enter_narrow, preferred_element_type=jnp.float32
    )
    query_grad = jnp.einsum(
        "jhts,jshd->jthd", grows, key_blocks, preferred_element_type=jnp.float32
    ) + forward_scale * jnp.einsum(
        "jthe,jhde->jthd", grad_blocks, enter_narrow, preferred_element_type=jnp.float32
    )
    key_grad = jnp.einsum(
        "jhts,jthd->jshd", grows, query_blocks, preferred_element_type=jnp.float32
    ) + backward_scale * jnp.einsum(
        "jshe,jhde->jshd", value_blocks, trail_narrow, preferred_element_type=jnp.float32
    )
    value_grad = jnp.einsum(
        "jhts,jthe->jshe", probs, grad_blocks, preferred_element_type=jnp.float32
    ) + backward_scale * jnp.einsum(
        "jshd,jhde->jshe", key_blocks, trail_narrow, preferred_element_type=jnp.float32
    )
    return tuple(
        (item.astype(jnp.bfloat16) for item in (attended, query_grad, key_grad, value_grad))
    )


def shards(queries, key_rows, value_rows, out_grad, log_decay):
    moved = (
        lax.all_to_all(queries, "inner", split_axis=1, concat_axis=0, tiled=True),
        lax.all_to_all(key_rows, "inner", split_axis=1, concat_axis=0, tiled=True),
        lax.all_to_all(value_rows, "inner", split_axis=1, concat_axis=0, tiled=True),
        lax.all_to_all(out_grad, "inner", split_axis=1, concat_axis=0, tiled=True),
        lax.all_to_all(log_decay, "inner", split_axis=1, concat_axis=0, tiled=True),
    )
    rows, local_heads = moved[4].shape
    blocks = rows // BLOCK
    shaped = tuple((item.reshape(blocks, BLOCK, local_heads, HEAD_SIZE) for item in moved[:4]))
    cumul, finals = block_setup(moved[4])
    parts, totals = local_states(shaped[0], shaped[1], shaped[2], shaped[3], cumul, finals)
    state_in, trail_in = chain_states(totals[0], totals[1], totals[2])
    entering, trailing = entries(parts, state_in, trail_in)
    results = block_results(
        shaped[0], shaped[1], shaped[2], shaped[3], cumul, finals, entering, trailing
    )
    flat = tuple((item.reshape(rows, local_heads * HEAD_SIZE) for item in results))
    returned = (
        lax.all_to_all(flat[0], "inner", split_axis=0, concat_axis=1, tiled=True),
        lax.all_to_all(flat[1], "inner", split_axis=0, concat_axis=1, tiled=True),
        lax.all_to_all(flat[2], "inner", split_axis=0, concat_axis=1, tiled=True),
        lax.all_to_all(flat[3], "inner", split_axis=0, concat_axis=1, tiled=True),
    )
    return (returned[0], returned[1], returned[2], returned[3])


def solution(mesh):
    return jax.shard_map(
        shards,
        mesh=mesh,
        in_specs=(
            P(("chain", "inner"), None),
            P(("chain", "inner"), None),
            P(("chain", "inner"), None),
            P(("chain", "inner"), None),
            P(("chain", "inner"), None),
        ),
        out_specs=(
            P(("chain", "inner"), None),
            P(("chain", "inner"), None),
            P(("chain", "inner"), None),
            P(("chain", "inner"), None),
        ),
        check_vma=False,
    )
```

profile of v0, /device:TPU:1, one launch (start us, length us, event | category | flops | bytes accessed | tf_op | source)
XLA Modules:
  0.0 393.3 jit_solution(15783194372114554354)
XLA Ops:
  1.9 8.6 %all-to-all-start.2 = ((bf16[128,32,1]{0,2,1:T(2,128)(2,1)}), bf16[128,32,1]{0,2,1:T(2,128)(2,1)S(1)}, u32[]{:S(2)}, u32[]{:S(2)}) async-start(bf16[128,32,1]{0,2,1:T(2,128)(2,1)} %copy.87), calls=%async_computation.2 | async-start | bytes 32768 | tf_op jit(solution)/shard_map/all_to_all | solution.py:145
  20.1 7.4 %all-to-all-start = ((bf16[128,32,128]{2,0,1:T(8,128)(2,1)}), bf16[128,32,128]{2,0,1:T(8,128)(2,1)S(1)}, u32[]{:S(2)}, u32[]{:S(2)}) async-start(bf16[128,32,128]{2,0,1:T(8,128)(2,1)} %copy.84), calls=%async_computation | async-start | bytes 2097152 | tf_op jit(solution)/shard_map/all_to_all | solution.py:141
  47.6 7.4 %all-to-all-start.5 = ((bf16[128,32,128]{2,0,1:T(8,128)(2,1)}), bf16[128,32,128]{2,0,1:T(8,128)(2,1)S(1)}, u32[]{:S(2)}, u32[]{:S(2)}) async-start(bf16[128,32,128]{2,0,1:T(8,128)(2,1)} %copy.98), calls=%async_computation.5 | async-start | bytes 2097152 | tf_op jit(solution)/shard_map/all_to_all | solution.py:144
  55.1 17.1 %all-reduce.42 = f32[8]{0:T(128)S(1)} all-reduce(f32[8]{0:T(128)S(1)} %bitcast_dynamic-update-slice_fusion), channel_id=1, replica_groups=mesh['chain'=8,'inner'=32] {'chain'}, use_global_device_ids=true, to_apply=%add.42 | all-reduce | flops 8 | bytes 64
  77.7 10.3 %all-to-all-start.1 = ((bf16[128,32,128]{2,0,1:T(8,128)(2,1)}), bf16[128,32,128]{2,0,1:T(8,128)(2,1)S(1)}, u32[]{:S(2)}, u32[]{:S(2)}) async-start(bf16[128,32,128]{2,0,1:T(8,128)(2,1)} %copy.86), calls=%async_computation.1 | async-start | bytes 2097152 | tf_op jit(solution)/shard_map/all_to_all | solution.py:142
  115.5 5.7 %pad.163 = f32[16,1,128,128]{3,2,0,1:T(8,128)} pad(f32[8,1,128,128]{3,2,0,1:T(8,128)} %add.386, f32[]{:T(128)} %constant.61.clone.1), padding=1_0_1x0_0_0x0_0_0x0_0_0 | pad | bytes 1572868 | tf_op jit(solution)/shard_map/pad | solution.py:35
  125.1 6.4 %pad.164 = f32[32,1,128,128]{3,2,0,1:T(8,128)} pad(f32[16,1,128,128]{3,2,0,1:T(8,128)S(1)} %pad_maximum_fusion.1, f32[]{:T(128)} %constant.61.clone.1), padding=0_1_1x0_0_0x0_0_0x0_0_0 | pad | bytes 3145732 | tf_op jit(solution)/shard_map/pad | solution.py:35
  131.6 6.4 %pad.208 = f32[31,1,128,128]{3,2,0,1:T(8,128)} pad(f32[16,1,128,128]{3,2,0,1:T(8,128)S(1)} %pad_maximum_fusion.1, f32[]{:T(128)} %constant.61.clone.1), padding=0_0_1x0_0_0x0_0_0x0_0_0 | pad | bytes 3080196 | tf_op jit(solution)/shard_map/slice | solution.py:41
  138.0 10.2 %pad.275 = f32[32,1,128,128]{3,2,0,1:T(8,128)} pad(f32[16,1,128,128]{3,2,0,1:T(8,128)} %add.388, f32[]{:T(128)} %constant.61.clone.1), padding=1_0_1x0_0_0x0_0_0x0_0_0 | pad | bytes 3145732
  149.1 19.3 %all_gather.12 = f32[8,1,128,128]{3,2,1,0:T(8,128)S(1)} all-gather(f32[1,1,128,128]{3,2,1,0:T(8,128)S(1)} %add_bitcast_fusion), channel_id=1, replica_groups=mesh['chain'=8,'inner'=32] {'chain'}, dimensions={0}, use_global_device_ids=true | all-gather | bytes 589824 | tf_op jit(solution)/shard_map/all_gather | solution.py:12
  168.4 8.9 %while.29 = (s32[]{:T(128)}, f32[1,128,128]{2,1,0:T(8,128)S(1)}, s32[]{:T(128)}, f32[8,1]{0,1:T(1,128)S(1)}, f32[8,1,128,128]{3,2,1,0:T(8,128)S(1)}, /*index=5*/s32[]{:T(128)}, s32[]{:T(128)}) while((s32[]{:T(128)}, f32[1,128,128]{2,1,0:T(8,128)S(1)}, s32[]{:T(128)}, f32[8,1]{0,1:T(1,128)S(1)}, f32[8,1,128,128]{3,2,1,0:T(8,128)S(1)}, ...), condition=%wide.region_3.4_spmd.clone, body=%wide.region_2.3_spmd.clone.sunk | while | flops 65540 | bytes 196725 | solution.py:24
  177.4 13.5 %all-to-all-start.3 = ((bf16[128,32,128]{2,0,1:T(8,128)(2,1)}), bf16[128,32,128]{2,0,1:T(8,128)(2,1)}, u32[]{:S(2)}, u32[]{:S(2)}) async-start(bf16[128,32,128]{2,0,1:T(8,128)(2,1)} %copy.90), calls=%async_computation.3 | async-start | bytes 2097152 | tf_op jit(solution)/shard_map/all_to_all | solution.py:143
  202.8 5.4 %all-to-all-done.3 = bf16[128,32,128]{2,0,1:T(8,128)(2,1)} async-done(((bf16[128,32,128]{2,0,1:T(8,128)(2,1)}), bf16[128,32,128]{2,0,1:T(8,128)(2,1)}, u32[]{:S(2)}, u32[]{:S(2)}) %all-to-all-start.3) | async-done | bytes 1048608 | tf_op jit(solution)/shard_map/all_to_all | solution.py:143
  237.9 5.7 %pad.142 = f32[16,1,128,128]{3,2,0,1:T(8,128)} pad(f32[8,1,128,128]{3,2,0,1:T(8,128)} %pad_maximum_fusion.2, f32[]{:T(128)} %constant.61.clone.1), padding=0_1_1x0_0_0x0_0_0x0_0_0 | pad | bytes 1572868 | tf_op jit(solution)/shard_map/pad | solution.py:34
  243.6 5.7 %pad.143 = f32[16,1,128,128]{3,2,0,1:T(8,128)} pad(f32[8,1,128,128]{3,2,0,1:T(8,128)} %add.355, f32[]{:T(128)} %constant.61.clone.1), padding=1_0_1x0_0_0x0_0_0x0_0_0 | pad | bytes 1572868 | tf_op jit(solution)/shard_map/pad | solution.py:34
  251.9 10.2 %pad.274 = f32[32,1,128,128]{3,2,0,1:T(8,128)} pad(f32[16,1,128,128]{3,2,0,1:T(8,128)} %add.357, f32[]{:T(128)} %constant.61.clone.1), padding=1_0_1x0_0_0x0_0_0x0_0_0 | pad | bytes 3145732
  265.2 10.2 %pad.144 = f32[32,1,128,128]{3,2,0,1:T(8,128)} pad(f32[16,1,128,128]{3,2,0,1:T(8,128)} %pad_maximum_fusion, f32[]{:T(128)} %constant.61.clone.1), padding=0_1_1x0_0_0x0_0_0x0_0_0 | pad | bytes 3145732 | tf_op jit(solution)/shard_map/pad | solution.py:34
  276.4 21.3 %all_gather.11 = f32[8,1,128,128]{3,2,1,0:T(8,128)} all-gather(f32[1,1,128,128]{3,2,1,0:T(8,128)S(1)} %add_bitcast_fusion.1), channel_id=1, replica_groups=mesh['chain'=8,'inner'=32] {'chain'}, dimensions={0}, use_global_device_ids=true | all-gather | bytes 589824 | tf_op jit(solution)/shard_map/all_gather | solution.py:12
  304.9 13.7 %all-to-all-start.7 = ((bf16[32,128,128]{2,1,0:T(8,128)(2,1)}), bf16[32,128,128]{2,1,0:T(8,128)(2,1)}, u32[]{:S(2)}, u32[]{:S(2)}) async-start(bf16[32,128,128]{2,1,0:T(8,128)(2,1)} %fusion.8), calls=%async_computation.7 | async-start | bytes 2097152 | tf_op jit(solution)/shard_map/all_to_all | solution.py:161
  318.6 14.6 %while.28 = (s32[]{:T(128)}, f32[1,128,128]{2,1,0:T(8,128)S(1)}, s32[]{:T(128)}, f32[8,1]{0,1:T(1,128)S(1)}, f32[8,1,128,128]{3,2,1,0:T(8,128)}, /*index=5*/s32[]{:T(128)}, s32[]{:T(128)}) while((s32[]{:T(128)}, f32[1,128,128]{2,1,0:T(8,128)S(1)}, s32[]{:T(128)}, f32[8,1]{0,1:T(1,128)S(1)}, f32[8,1,128,128]{3,2,1,0:T(8,128)}, ...), condition=%wide.region_1.2_spmd.clone, body=%wide.region_0.1_spmd.clone.sunk | while | flops 65540 | bytes 196725 | solution.py:24
  333.2 6.4 %pad.206 = f32[31,1,128,128]{3,2,0,1:T(8,128)} pad(f32[16,1,128,128]{3,2,0,1:T(8,128)S(1)} %copy-done.8, f32[]{:T(128)} %constant.61.clone.1), padding=0_0_1x0_0_0x0_0_0x0_0_0 | pad | bytes 3080196 | tf_op jit(solution)/shard_map/slice | solution.py:39
  345.4 7.4 %all-to-all-start.6 = ((bf16[32,128,128]{2,1,0:T(8,128)(2,1)}), bf16[32,128,128]{2,1,0:T(8,128)(2,1)}, u32[]{:S(2)}, u32[]{:S(2)}) async-start(bf16[32,128,128]{2,1,0:T(8,128)(2,1)} %fusion.7), calls=%async_computation.6 | async-start | bytes 2097152 | tf_op jit(solution)/shard_map/all_to_all | solution.py:160
  356.4 13.6 %all-to-all-done.6 = bf16[32,128,128]{2,1,0:T(8,128)(2,1)} async-done(((bf16[32,128,128]{2,1,0:T(8,128)(2,1)}), bf16[32,128,128]{2,1,0:T(8,128)(2,1)}, u32[]{:S(2)}, u32[]{:S(2)}) %all-to-all-start.6) | async-done | bytes 1048608 | tf_op jit(solution)/shard_map/all_to_all | solution.py:160
  382.9 8.5 %all-to-all-done.4 = bf16[32,128,128]{2,1,0:T(8,128)(2,1)S(1)} async-done(((bf16[32,128,128]{2,1,0:T(8,128)(2,1)}), bf16[32,128,128]{2,1,0:T(8,128)(2,1)S(1)}, u32[]{:S(2)}, u32[]{:S(2)}) %all-to-all-start.4) | async-done | bytes 1048608 | tf_op jit(solution)/shard_map/all_to_all | solution.py:159
  (283 shorter events, 164.7 us)
Async XLA Ops:
  1.9 18.2 %all-to-all-start.2 = ((bf16[128,32,1]{0,2,1:T(2,128)(2,1)}), bf16[128,32,1]{0,2,1:T(2,128)(2,1)S(1)}, u32[]{:S(2)}, u32[]{:S(2)}) async-start(bf16[128,32,1]{0,2,1:T(2,128)(2,1)} %copy.87), calls=%async_computation.2 | async-start | bytes 32768 | tf_op jit(solution)/shard_map/all_to_all | solution.py:145
  20.1 27.4 %all-to-all-start = ((bf16[128,32,128]{2,0,1:T(8,128)(2,1)}), bf16[128,32,128]{2,0,1:T(8,128)(2,1)S(1)}, u32[]{:S(2)}, u32[]{:S(2)}) async-start(bf16[128,32,128]{2,0,1:T(8,128)(2,1)} %copy.84), calls=%async_computation | async-start | bytes 2097152 | tf_op jit(solution)/shard_map/all_to_all | solution.py:141
  47.6 30.1 %all-to-all-start.5 = ((bf16[128,32,128]{2,0,1:T(8,128)(2,1)}), bf16[128,32,128]{2,0,1:T(8,128)(2,1)S(1)}, u32[]{:S(2)}, u32[]{:S(2)}) async-start(bf16[128,32,128]{2,0,1:T(8,128)(2,1)} %copy.98), calls=%async_computation.5 | async-start | bytes 2097152 | tf_op jit(solution)/shard_map/all_to_all | solution.py:144
  77.7 11.8 %copy-start = (bf16[128,32,128]{2,0,1:T(8,128)(2,1)}, bf16[128,32,128]{2,0,1:T(8,128)(2,1)S(1)}, u32[]{:S(2)}) copy-start(bf16[128,32,128]{2,0,1:T(8,128)(2,1)S(1)} %all-to-all-done.5) | copy-start | bytes 3145732
  77.7 99.7 %all-to-all-start.1 = ((bf16[128,32,128]{2,0,1:T(8,128)(2,1)}), bf16[128,32,128]{2,0,1:T(8,128)(2,1)S(1)}, u32[]{:S(2)}, u32[]{:S(2)}) async-start(bf16[128,32,128]{2,0,1:T(8,128)(2,1)} %copy.86), calls=%async_computation.1 | async-start | bytes 2097152 | tf_op jit(solution)/shard_map/all_to_all | solution.py:142
  92.4 11.0 %slice-start.1 = ((f32[8,1,128,128]{3,2,0,1:T(8,128)}), f32[1,1,128,128]{3,2,0,1:T(8,128)S(1)}, s32[]{:S(2)}) async-start(f32[8,1,128,128]{3,2,0,1:T(8,128)} %copy-done.15), calls=%async_computation.10 | async-start | bytes 131072 | tf_op jit(solution)/shard_map/slice | solution.py:35
  98.4 11.5 %copy-start.29 = (f32[7]{0:T(128)S(1)}, f32[7]{0:T(128)}, u32[]{:S(2)}) copy-start(f32[7]{0:T(128)} %get-tuple-element.297) | copy-start | bytes 88
  104.1 7.1 %copy-start.22 = (f32[1,1,128,128]{3,2,0,1:T(8,128)S(1)}, f32[1,1,128,128]{3,2,0,1:T(8,128)}, u32[]{:S(2)}) copy-start(f32[1,1,128,128]{3,2,0,1:T(8,128)} %slice.456) | copy-start | bytes 196612
  115.5 8.1 %copy-start.24 = (f32[15]{0:T(128)S(1)}, f32[15]{0:T(128)}, u32[]{:S(2)}) copy-start(f32[15]{0:T(128)} %get-tuple-element.295) | copy-start | bytes 184
  138.0 30.4 %copy-start.33 = (f32[8]{0:T(128)S(1)}, f32[8]{0:T(128)}, u32[]{:S(2)}) copy-start(f32[8]{0:T(128)} %reverse.12) | copy-start | bytes 100
  177.4 13.5 %copy-start.3 = (bf16[128,32,128]{2,0,1:T(8,128)(2,1)}, bf16[128,32,128]{2,0,1:T(8,128)(2,1)S(1)}, u32[]{:S(2)}) copy-start(bf16[128,32,128]{2,0,1:T(8,128)(2,1)S(1)} %all-to-all-done.1) | copy-start | bytes 3145732
  177.4 30.7 %all-to-all-start.3 = ((bf16[128,32,128]{2,0,1:T(8,128)(2,1)}), bf16[128,32,128]{2,0,1:T(8,128)(2,1)}, u32[]{:S(2)}, u32[]{:S(2)}) async-start(bf16[128,32,128]{2,0,1:T(8,128)(2,1)} %copy.90), calls=%async_computation.3 | async-start | bytes 2097152 | tf_op jit(solution)/shard_map/all_to_all | solution.py:143
  208.1 96.7 %all-to-all-start.8 = ((bf16[32,128,128]{2,1,0:T(8,128)(2,1)}), bf16[32,128,128]{2,1,0:T(8,128)(2,1)}, u32[]{:S(2)}, u32[]{:S(2)}) async-start(bf16[32,128,128]{2,1,0:T(8,128)(2,1)} %fusion.9), calls=%async_computation.8 | async-start | bytes 2097152 | tf_op jit(solution)/shard_map/all_to_all | solution.py:162
  218.0 9.9 %copy-start.26 = (f32[3]{0:T(128)S(1)}, f32[3]{0:T(128)}, u32[]{:S(2)}) copy-start(f32[3]{0:T(128)} %get-tuple-element.317) | copy-start | bytes 40
  218.1 11.0 %slice-start.2 = ((f32[8,1,128,128]{3,2,0,1:T(8,128)}), f32[1,1,128,128]{3,2,0,1:T(8,128)S(1)}, s32[]{:S(2)}) async-start(f32[8,1,128,128]{3,2,0,1:T(8,128)} %copy-done.16), calls=%async_computation.11 | async-start | bytes 131072 | tf_op jit(solution)/shard_map/slice | solution.py:34
  224.1 11.5 %copy-start.28 = (f32[7]{0:T(128)S(1)}, f32[7]{0:T(128)}, u32[]{:S(2)}) copy-start(f32[7]{0:T(128)} %get-tuple-element.315) | copy-start | bytes 88
  229.8 7.2 %slice-start = ((f32[16,1,128,128]{3,2,0,1:T(8,128)}), f32[1,1,128,128]{3,2,0,1:T(8,128)S(1)}, s32[]{:S(2)}) async-start(f32[16,1,128,128]{3,2,0,1:T(8,128)} %copy-done.12), calls=%async_computation.9 | async-start | bytes 131072 | tf_op jit(solution)/shard_map/slice | solution.py:34
  251.9 10.2 %copy-start.23 = (f32[15]{0:T(128)S(1)}, f32[15]{0:T(128)}, u32[]{:S(2)}) copy-start(f32[15]{0:T(128)} %get-tuple-element.313) | copy-start | bytes 184
  304.8 13.7 %copy-start.32 = (f32[8]{0:T(128)S(1)}, f32[8]{0:T(128)}, u32[]{:S(2)}) copy-start(f32[8]{0:T(128)} %copy-done.31) | copy-start | bytes 100
  304.8 28.4 %copy-start.8 = (f32[16,1,128,128]{3,2,0,1:T(8,128)S(1)}, f32[16,1,128,128]{3,2,0,1:T(8,128)}, u32[]{:S(2)}) copy-start(f32[16,1,128,128]{3,2,0,1:T(8,128)} %pad_maximum_fusion) | copy-start | bytes 3145732
  304.9 40.5 %all-to-all-start.7 = ((bf16[32,128,128]{2,1,0:T(8,128)(2,1)}), bf16[32,128,128]{2,1,0:T(8,128)(2,1)}, u32[]{:S(2)}, u32[]{:S(2)}) async-start(bf16[32,128,128]{2,1,0:T(8,128)(2,1)} %fusion.8), calls=%async_computation.7 | async-start | bytes 2097152 | tf_op jit(solution)/shard_map/all_to_all | solution.py:161
  318.5 21.1 %copy-start.5 = (bf16[128,32,128]{2,0,1:T(8,128)(2,1)S(1)}, bf16[128,32,128]{2,0,1:T(8,128)(2,1)}, u32[]{:S(2)}) copy-start(bf16[128,32,128]{2,0,1:T(8,128)(2,1)} %copy-done.3) | copy-start | bytes 3145732
  345.4 24.7 %all-to-all-start.6 = ((bf16[32,128,128]{2,1,0:T(8,128)(2,1)}), bf16[32,128,128]{2,1,0:T(8,128)(2,1)}, u32[]{:S(2)}, u32[]{:S(2)}) async-start(bf16[32,128,128]{2,1,0:T(8,128)(2,1)} %fusion.7), calls=%async_computation.6 | async-start | bytes 2097152 | tf_op jit(solution)/shard_map/all_to_all | solution.py:160
  370.1 21.3 %all-to-all-start.4 = ((bf16[32,128,128]{2,1,0:T(8,128)(2,1)}), bf16[32,128,128]{2,1,0:T(8,128)(2,1)S(1)}, u32[]{:S(2)}, u32[]{:S(2)}) async-start(bf16[32,128,128]{2,1,0:T(8,128)(2,1)} %fusion.6), calls=%async_computation.4 | async-start | bytes 2097152 | tf_op jit(solution)/shard_map/all_to_all | solution.py:159
  (22 other events, 41.4 us)
where the time goes:
time: 399 us; the launch traced here: 393 us
  local copies, waits for them, and re-layouts  142 us (36%)
  starting transfers between devices  76.9 us (19%)
  other arithmetic  57.9 us (15%)
  blocking collectives  57.7 us (14%)
  waiting for transfers between devices  27.5 us (7%)
  matrix products  23.3 us (6%)
  between operations  7.89 us (2%)
    all_gather x2, blocking collectives, carried_in(): pieces = jax.tree.map(lambda part: lax.all_gather(part, axis), value)  40.6 us
    unnamed x82, local copies, waits for them, and re-layouts  37.6 us
    pad x15, local copies, waits for them, and re-layouts, prefixes(): fwd_sum, fwd_state = lax.associative_scan(combine, (sums, forward_terms))  33.4 us
    pad x15, local copies, waits for them, and re-layouts, prefixes(): lax.associative_scan(combine, (sums, backward_terms), reverse=True)  27.4 us
    unnamed x1, blocking collectives  17.1 us
    select_n x14, other arithmetic, hop(): jnp.where(position < mine, new, old)  14.9 us
    all_to_all x1, starting transfers between devices, shards(): lax.all_to_all(flat[2], 'inner', split_axis=0, concat_axis=1, tiled=True)  13.7 us
    all_to_all x1, waiting for transfers between devices, shards(): lax.all_to_all(flat[1], 'inner', split_axis=0, concat_axis=1, tiled=True)  13.6 us
  transfers between devices with their start and end apart: 9, of which 3 were waited for; matrix products, arithmetic and copies ran while one was open for 54% of the time, Pallas kernels for 0%

commit v1 on v0

v1 whole, which is shorter than its diff:
```python
import jax
import jax.numpy as jnp
from jax import lax
from jax.experimental import pallas as pl
from jax.experimental.pallas import tpu as pltpu
from jax.sharding import Mesh, PartitionSpec as P

HEAD = 128
BLOCK = 128
HALF_HEADS = 16
STEPS = 4
PER_STEP = HALF_HEADS // STEPS
PART = HEAD // 2
TAIL = 16
AXES = ("zh", "zl", "y", "x", "core")
GROUP = ("zl", "y", "x")

F32 = jnp.float32
BF16 = jnp.bfloat16
VMEM_LIMIT = 48 * 1024 * 1024


def dot(left, right, left_dim, right_dim):
    return lax.dot_general(
        left, right, (((left_dim,), (right_dim,)), ((), ())), preferred_element_type=F32
    )


def pack_decay(value):
    full = jnp.broadcast_to(value, (TAIL, HEAD))
    high = full.astype(BF16)
    rest = full - high.astype(F32)
    middle = rest.astype(BF16)
    low = (rest - middle.astype(F32)).astype(BF16)
    row = lax.broadcasted_iota(jnp.int32, (TAIL, HEAD), 0)
    chosen = jnp.where(
        row == 0, high.astype(F32), jnp.where(row == 1, middle.astype(F32), low.astype(F32))
    )
    return chosen.astype(BF16)


def unpack_decay(tile):
    rows = tile.astype(F32)
    return rows[0:1] + rows[1:2] + rows[2:3]


def lower_triangle():
    at = lax.broadcasted_iota(jnp.int32, (BLOCK, BLOCK), 0)
    before = lax.broadcasted_iota(jnp.int32, (BLOCK, BLOCK), 1)
    return at >= before


def half_decay(decay_ref, half):
    decay = decay_ref[...].astype(F32)
    return jnp.where(half == 0, decay[:, :HALF_HEADS], decay[:, HALF_HEADS:]).astype(BF16)


def set_scales(decay_ref, half, fwd_ref, bwd_ref, final_ref, cols_ref=None, rows_ref=None):
    decay = half_decay(decay_ref, half)
    triangle = lower_triangle().astype(F32).astype(BF16)
    cumul = dot(triangle, decay, 1, 0)
    finals = cumul[BLOCK - 1 : BLOCK, :]
    fwd = jnp.exp(cumul)
    bwd = jnp.exp(finals - cumul)
    for step in range(STEPS):
        heads = slice(step * PER_STEP, (step + 1) * PER_STEP)
        fwd_ref[step] = fwd[:, heads]
        bwd_ref[step] = bwd[:, heads]
        final_ref[step] = jnp.broadcast_to(finals[:, heads], (8, PER_STEP))
        if cols_ref is not None:
            cols_ref[step] = cumul[:, heads]
    if rows_ref is not None:
        rows = dot(decay, triangle, 0, 1)
        for step in range(STEPS):
            rows_ref[step] = rows[step * PER_STEP : (step + 1) * PER_STEP]


def head_states(query, key, value, grad, fwd, bwd):
    scaled_key = (key.astype(F32) * bwd).astype(BF16)
    scaled_query = (query.astype(F32) * fwd).astype(BF16)
    return dot(scaled_key, value, 0, 0), dot(scaled_query, grad, 0, 0)


def send_states(
    half_ref, decay_ref, query_ref, key_ref, value_ref, grad_ref, out_ref, fwd_ref, bwd_ref, final_ref
):
    step = pl.program_id(0)

    @pl.when(step == 0)
    def _():
        set_scales(decay_ref, half_ref[0], fwd_ref, bwd_ref, final_ref)

    fwd = fwd_ref[step]
    bwd = bwd_ref[step]
    finals = final_ref[step]
    for head in range(PER_STEP):
        cols = slice(head * HEAD, (head + 1) * HEAD)
        one = slice(head, head + 1)
        kv, qd = head_states(
            query_ref[:, cols], key_ref[:, cols], value_ref[:, cols], grad_ref[:, cols],
            fwd[:, one], bwd[:, one],
        )
        out_ref[head, 0:HEAD, :] = kv.astype(BF16)
        out_ref[head, HEAD : 2 * HEAD, :] = qd.astype(BF16)
        out_ref[head, 2 * HEAD :, :] = pack_decay(finals[0:1, one])


def keep_states(
    half_ref, decay_ref, query_ref, key_ref, value_ref, grad_ref, other_ref,
    own_ref, pair_ref, fwd_ref, bwd_ref, final_ref,
):
    step = pl.program_id(0)
    first = half_ref[0] == 0

    @pl.when(step == 0)
    def _():
        set_scales(decay_ref, half_ref[0], fwd_ref, bwd_ref, final_ref)

    fwd = fwd_ref[step]
    bwd = bwd_ref[step]
    finals = final_ref[step]
    for head in range(PER_STEP):
        cols = slice(head * HEAD, (head + 1) * HEAD)
        one = slice(head, head + 1)
        kv, qd = head_states(
            query_ref[:, cols], key_ref[:, cols], value_ref[:, cols], grad_ref[:, cols],
            fwd[:, one], bwd[:, one],
        )
        mine = jnp.broadcast_to(finals[0:1, one], (1, HEAD))
        theirs = unpack_decay(other_ref[head, 2 * HEAD :, :])
        own_ref[head, 0:HEAD, :] = kv.astype(BF16)
        own_ref[head, HEAD : 2 * HEAD, :] = qd.astype(BF16)
        own_ref[head, 2 * HEAD :, :] = pack_decay(finals[0:1, one])
        other_kv = other_ref[head, 0:HEAD, :].astype(F32)
        other_qd = other_ref[head, HEAD : 2 * HEAD, :].astype(F32)
        decay_mine = jnp.exp(mine)
        decay_theirs = jnp.exp(theirs)
        unit = jnp.ones_like(mine)
        pair_kv = jnp.where(first, decay_theirs, unit) * kv + jnp.where(first, unit, decay_mine) * other_kv
        pair_qd = jnp.where(first, unit, decay_theirs) * qd + jnp.where(first, decay_mine, unit) * other_qd
        pair_kv = pair_kv.astype(BF16)
        pair_qd = pair_qd.astype(BF16)
        tail = pack_decay(mine + theirs)
        for part in range(2):
            rows = slice(part * PART, (part + 1) * PART)
            pair_ref[2 * head + part, 0:PART, :] = pair_kv[rows]
            pair_ref[2 * head + part, PART : 2 * PART, :] = pair_qd[rows]
            pair_ref[2 * head + part, 2 * PART :, :] = tail


def group_total(pieces_ref, out_ref):
    count = pieces_ref.shape[0]
    zero = jnp.zeros((PART, HEAD), F32)

    def hop(at, carry):
        state, trail, total = carry
        back = count - 1 - at
        decay = unpack_decay(pieces_ref[at, 2 * PART :, :])
        decay_back = unpack_decay(pieces_ref[back, 2 * PART :, :])
        state = jnp.exp(decay) * state + pieces_ref[at, 0:PART, :].astype(F32)
        trail = jnp.exp(decay_back) * trail + pieces_ref[back, PART : 2 * PART, :].astype(F32)
        return state, trail, total + decay

    state, trail, total = lax.fori_loop(
        0, count, hop, (zero, zero, jnp.zeros((1, HEAD), F32)), unroll=4
    )
    out_ref[0:PART, :] = state.astype(BF16)
    out_ref[PART : 2 * PART, :] = trail.astype(BF16)
    out_ref[2 * PART :, :] = pack_decay(total)


def group_entries(index_ref, pieces_ref, one_ref, two_ref, three_ref, out_ref):
    count = pieces_ref.shape[0]
    place = index_ref[0]
    state = jnp.zeros((PART, HEAD), F32)
    trail = jnp.zeros((PART, HEAD), F32)
    for distance, ref in ((3, three_ref), (2, two_ref), (1, one_ref)):
        longer = jnp.exp(unpack_decay(ref[2 * PART :, :])) * state + ref[0:PART, :].astype(F32)
        state = jnp.where(place >= distance, longer, state)
    for distance, ref in ((1, one_ref), (2, two_ref), (3, three_ref)):
        longer = jnp.exp(unpack_decay(ref[2 * PART :, :])) * trail + ref[PART : 2 * PART, :].astype(F32)
        trail = jnp.where(place < distance, longer, trail)

    def hop(at, carry):
        state, trail = carry
        back = count - 1 - at
        out_ref[at, 0:PART, :] = state.astype(BF16)
        out_ref[back, PART : 2 * PART, :] = trail.astype(BF16)
        decay = unpack_decay(pieces_ref[at, 2 * PART :, :])
        decay_back = unpack_decay(pieces_ref[back, 2 * PART :, :])
        state = jnp.exp(decay) * state + pieces_ref[at, 0:PART, :].astype(F32)
        trail = jnp.exp(decay_back) * trail + pieces_ref[back, PART : 2 * PART, :].astype(F32)
        return state, trail

    lax.fori_loop(0, count, hop, (state, trail), unroll=4)


def other_entries(half_ref, own_ref, pair_ref, out_ref):
    first = half_ref[0] == 0
    for head in range(PER_STEP):
        decay = jnp.exp(unpack_decay(own_ref[head, 2 * HEAD :, :]))
        for part in range(2):
            rows = slice(part * PART, (part + 1) * PART)
            qd_rows = slice(HEAD + part * PART, HEAD + (part + 1) * PART)
            state = pair_ref[2 * head + part, 0:PART, :].astype(F32)
            trail = pair_ref[2 * head + part, PART : 2 * PART, :].astype(F32)
            later = decay * state + own_ref[head, rows, :].astype(F32)
            earlier = decay * trail + own_ref[head, qd_rows, :].astype(F32)
            out_ref[head, rows, :] = jnp.where(first, later, state).astype(BF16)
            out_ref[head, qd_rows, :] = jnp.where(first, trail, earlier).astype(BF16)


def head_results(query, key, value, grad, col, row, fwd, bwd, entering, trailing, lower):
    weights = jnp.exp(jnp.where(lower, col - row, -jnp.inf))
    probs = (dot(query, key, 1, 1) * weights).astype(BF16)
    grows = (dot(grad, value, 1, 1) * weights).astype(BF16)
    attended = dot(probs, value, 1, 0) + fwd * dot(query, entering, 1, 0)
    query_grad = dot(grows, key, 1, 0) + fwd * dot(grad, entering, 1, 1)
    key_grad = dot(grows, query, 0, 0) + bwd * dot(value, trailing, 1, 1)
    value_grad = dot(probs, grad, 0, 0) + bwd * dot(key, trailing, 1, 0)
    return attended, query_grad, key_grad, value_grad


def own_results(
    half_ref, decay_ref, query_ref, key_ref, value_ref, grad_ref, pair_ref, other_ref,
    att_ref, qg_ref, kg_ref, vg_ref, fwd_ref, bwd_ref, final_ref, cols_ref, rows_ref,
):
    step = pl.program_id(0)
    first = half_ref[0] == 0

    @pl.when(step == 0)
    def _():
        set_scales(decay_ref, half_ref[0], fwd_ref, bwd_ref, final_ref, cols_ref, rows_ref)

    lower = lower_triangle()
    for head in range(PER_STEP):
        cols = slice(head * HEAD, (head + 1) * HEAD)
        one = slice(head, head + 1)
        decay = jnp.exp(unpack_decay(other_ref[head, 2 * HEAD :, :]))
        state = jnp.concatenate(
            [pair_ref[2 * head, 0:PART, :], pair_ref[2 * head + 1, 0:PART, :]], axis=0
        ).astype(F32)
        trail = jnp.concatenate(
            [pair_ref[2 * head, PART : 2 * PART, :], pair_ref[2 * head + 1, PART : 2 * PART, :]], axis=0
        ).astype(F32)
        later = decay * state + other_ref[head, 0:HEAD, :].astype(F32)
        earlier = decay * trail + other_ref[head, HEAD : 2 * HEAD, :].astype(F32)
        results = head_results(
            query_ref[:, cols], key_ref[:, cols], value_ref[:, cols], grad_ref[:, cols],
            cols_ref[step][:, one], rows_ref[step][one], fwd_ref[step][:, one], bwd_ref[step][:, one],
            jnp.where(first, state, later).astype(BF16), jnp.where(first, earlier, trail).astype(BF16),
            lower,
        )
        for ref, item in zip((att_ref, qg_ref, kg_ref, vg_ref), results):
            ref[:, cols] = item.astype(BF16)


def other_results(
    half_ref, decay_ref, query_ref, key_ref, value_ref, grad_ref, entry_ref, a_ref, b_ref, c_ref, d_ref,
    att_ref, qg_ref, kg_ref, vg_ref, fwd_ref, bwd_ref, final_ref, cols_ref, rows_ref,
):
    step = pl.program_id(0)

    @pl.when(step == 0)
    def _():
        set_scales(decay_ref, half_ref[0], fwd_ref, bwd_ref, final_ref, cols_ref, rows_ref)

    lower = lower_triangle()
    for head in range(PER_STEP):
        cols = slice(head * HEAD, (head + 1) * HEAD)
        one = slice(head, head + 1)
        results = head_results(
            query_ref[:, cols], key_ref[:, cols], value_ref[:, cols], grad_ref[:, cols],
            cols_ref[step][:, one], rows_ref[step][one], fwd_ref[step][:, one], bwd_ref[step][:, one],
            entry_ref[head, 0:HEAD, :], entry_ref[head, HEAD : 2 * HEAD, :], lower,
        )
        for ref, item in zip((att_ref, qg_ref, kg_ref, vg_ref), results):
            ref[:, cols] = item.astype(BF16)


def whole(shape):
    return pl.BlockSpec(shape, lambda *_: (0,) * len(shape))


def heads_of_half():
    return pl.BlockSpec((BLOCK, PER_STEP * HEAD), lambda step, half: (0, half[0] * STEPS + step))


def by_step(*shape):
    return pl.BlockSpec(shape, lambda step, half: (step,) + (0,) * (len(shape) - 1))


SCALES = (
    pltpu.VMEM((STEPS, BLOCK, PER_STEP), F32),
    pltpu.VMEM((STEPS, BLOCK, PER_STEP), F32),
    pltpu.VMEM((STEPS, 8, PER_STEP), F32),
)
CUMULS = (
    pltpu.VMEM((STEPS, BLOCK, PER_STEP), F32),
    pltpu.VMEM((STEPS, PER_STEP, BLOCK), F32),
)


def call(kernel, half, operands, in_specs, out_specs, out_shape, scratch=(), grid=(STEPS,), aliases=None):
    return pl.pallas_call(
        kernel,
        out_shape=out_shape,
        grid_spec=pltpu.PrefetchScalarGridSpec(
            num_scalar_prefetch=1, grid=grid, in_specs=in_specs, out_specs=out_specs,
            scratch_shapes=list(scratch),
        ),
        input_output_aliases=aliases or {},
        compiler_params=pltpu.CompilerParams(vmem_limit_bytes=VMEM_LIMIT),
    )(half, *operands)


def shards(queries, key_rows, value_rows, out_grad, log_decay):
    core = lax.axis_index("core")
    mine = core.reshape(1).astype(jnp.int32)
    theirs = 1 - mine
    place = lax.axis_index("zh").reshape(1).astype(jnp.int32)
    rows = (queries, key_rows, value_rows, out_grad)
    row_specs = [whole((BLOCK, 2 * HALF_HEADS))] + [heads_of_half() for _ in rows]
    state_rows = 2 * HEAD + TAIL
    piece_rows = 2 * PART + TAIL
    swap = [(0, 1), (1, 0)]

    sent = call(
        send_states, theirs, (log_decay,) + rows, row_specs, by_step(PER_STEP, state_rows, HEAD),
        jax.ShapeDtypeStruct((HALF_HEADS, state_rows, HEAD), BF16), SCALES,
    )
    other = lax.ppermute(sent, "core", swap)
    own, pairs = call(
        keep_states, mine, (log_decay,) + rows + (other,),
        row_specs + [by_step(PER_STEP, state_rows, HEAD)],
        [by_step(PER_STEP, state_rows, HEAD), by_step(2 * PER_STEP, piece_rows, HEAD)],
        [
            jax.ShapeDtypeStruct((HALF_HEADS, state_rows, HEAD), BF16),
            jax.ShapeDtypeStruct((2 * HALF_HEADS, piece_rows, HEAD), BF16),
        ],
        SCALES,
    )
    pieces = lax.all_to_all(pairs, GROUP, split_axis=0, concat_axis=0, tiled=True)
    total = pl.pallas_call(
        group_total,
        out_shape=jax.ShapeDtypeStruct((piece_rows, HEAD), BF16),
        compiler_params=pltpu.CompilerParams(vmem_limit_bytes=VMEM_LIMIT),
    )(pieces)
    size = lax.axis_size("zh")
    moved = [
        lax.ppermute(total, "zh", [(at, (at + distance) % size) for at in range(size)])
        for distance in (1, 2, 3)
    ]
    entries = call(
        group_entries, place, (pieces, *moved),
        [whole((2 * HALF_HEADS, piece_rows, HEAD))] + [whole((piece_rows, HEAD))] * 3,
        whole((2 * HALF_HEADS, 2 * PART, HEAD)),
        jax.ShapeDtypeStruct((2 * HALF_HEADS, 2 * PART, HEAD), BF16), grid=(1,),
    )
    pair_entries = lax.all_to_all(entries, GROUP, split_axis=0, concat_axis=0, tiled=True)
    leaving = call(
        other_entries, mine, (own, pair_entries),
        [by_step(PER_STEP, state_rows, HEAD), by_step(2 * PER_STEP, 2 * PART, HEAD)],
        by_step(PER_STEP, 2 * HEAD, HEAD),
        jax.ShapeDtypeStruct((HALF_HEADS, 2 * HEAD, HEAD), BF16),
    )
    arrived = lax.ppermute(leaving, "core", swap)
    shapes = [jax.ShapeDtypeStruct(queries.shape, BF16)] * 4
    results = call(
        own_results, mine, (log_decay,) + rows + (pair_entries, other),
        row_specs + [by_step(2 * PER_STEP, 2 * PART, HEAD), by_step(PER_STEP, state_rows, HEAD)],
        [heads_of_half()] * 4, shapes, SCALES + CUMULS,
    )
    results = call(
        other_results, theirs, (log_decay,) + rows + (arrived,) + tuple(results),
        row_specs + [by_step(PER_STEP, 2 * HEAD, HEAD)] + [pl.BlockSpec(memory_space=pl.ANY)] * 4,
        [heads_of_half()] * 4, shapes, SCALES + CUMULS, aliases={7: 0, 8: 1, 9: 2, 10: 3},
    )
    return tuple(results)


def solution(mesh):
    chain, inner = mesh.devices.shape
    grid = Mesh(mesh.devices.reshape(chain // 2, 2, 4, 4, inner // 16), AXES)
    spec = P(AXES, None)
    return jax.shard_map(
        shards, mesh=grid, in_specs=(spec,) * 5, out_specs=(spec,) * 4, check_vma=False
    )
```

time: 399 us -> 97.4 us (0.24); the launches traced: 393 us -> 96.8 us
  local copies, waits for them, and re-layouts: 142 us -> 9.04 us
  starting transfers between devices: 76.9 us -> 16.3 us
  other arithmetic: 57.9 us -> 0 us
  matrix products: 23.3 us -> 0 us
  Pallas kernels: 0 us -> 22.4 us
  waiting for transfers between devices: 27.5 us -> 5.95 us
  blocking collectives: 57.7 us -> 42.4 us
  between operations: 7.89 us -> 0.71 us
    all_to_all x9 -> x0, starting transfers between devices: 76.9 us -> none  [the longest x1 13.7 us: shards(): lax.all_to_all(flat[2], 'inner', split_axis=0, concat_axis=1, tiled=True)]
    pad x30 -> x0, local copies, waits for them, and re-layouts: 60.8 us -> none  [the longest x15 33.4 us: prefixes(): fwd_sum, fwd_state = lax.associative_scan(combine, (sums, forward_terms))]
    all_to_all x0 -> x2, blocking collectives: none -> 42.4 us  [the longest x1 24.8 us: shards(): lax.all_to_all(pairs, GROUP, split_axis=0, concat_axis=0, tiled=True)]
    all_gather x2 -> x0, blocking collectives: 40.6 us -> none  [carried_in(): pieces = jax.tree.map(lambda part: lax.all_gather(part, axis), value)]
    add x50 -> x0, other arithmetic: 32.1 us -> none  [the longest x10 10.7 us: prefixes(): lax.associative_scan(combine, (sums, backward_terms), reverse=True)]
    unnamed x82 -> x29, local copies, waits for them, and re-layouts: 37.6 us -> 9.04 us
    all_to_all x9 -> x0, waiting for transfers between devices: 27.5 us -> none  [the longest x1 13.6 us: shards(): lax.all_to_all(flat[1], 'inner', split_axis=0, concat_axis=1, tiled=True)]
    dot_general x13 -> x0, matrix products: 23.3 us -> none  [the longest x1 3.28 us: block_results(): jnp.einsum('jshe,jhde->jshd', value_blocks, trail_narrow, preferred_eleme...]
  transfers between devices with their start and end apart: 9 -> 5, of which waited for: 3 -> 2; matrix products, arithmetic and copies ran while one was open for 54% -> 0% of each run, Pallas kernels for 0% -> 7%
where the time goes in v1:
time: 97.4 us; the launch traced here: 96.8 us
  blocking collectives  42.4 us (44%)
  Pallas kernels  22.4 us (23%)
  starting transfers between devices  16.3 us (17%)
  local copies, waits for them, and re-layouts  9.04 us (9%)
  waiting for transfers between devices  5.95 us (6%)
    all_to_all x1, blocking collectives, shards(): lax.all_to_all(pairs, GROUP, split_axis=0, concat_axis=0, tiled=True)  24.8 us
    pallas_call x6, Pallas kernels, call(): pl.pallas_call(kernel, out_shape=out_shape, grid_spec=pltpu.PrefetchScala...  22 us
    all_to_all x1, blocking collectives, shards(): lax.all_to_all(entries, GROUP, split_axis=0, concat_axis=0, tiled=True)  17.6 us
    unnamed x29, local copies, waits for them, and re-layouts  9.04 us
    ppermute x3, starting transfers between devices, shards(): lax.ppermute(total, 'zh', [(at, (at + distance) % size) for at in range(s...  8.38 us
    ppermute x1, starting transfers between devices, shards(): arrived = lax.ppermute(leaving, 'core', swap)  4.62 us
    ppermute x3, waiting for transfers between devices, shards(): lax.ppermute(total, 'zh', [(at, (at + distance) % size) for at in range(s...  3.56 us
    ppermute x1, starting transfers between devices, shards(): other = lax.ppermute(sent, 'core', swap)  3.33 us
  transfers between devices with their start and end apart: 5, of which 2 were waited for; matrix products, arithmetic and copies ran while one was open for 0% of the time, Pallas kernels for 7%

profile of v1, /device:TPU:1, one launch (start us, length us, event | category | flops | bytes accessed | tf_op | source)
XLA Modules:
  0.0 96.8 jit_solution(7422538784161493718)
XLA Ops:
  0.6 0.8 copy.16.decay_ref
  1.5 1.2 %copy-done = bf16[128,4096]{1,0:T(8,128)(2,1)S(1)} copy-done((bf16[128,4096]{1,0:T(8,128)(2,1)S(1)}, bf16[128,4096]{1,0:T(8,128)(2,1)}, u32[]{:S(2)}) %copy-start) | copy-done | bytes 1048600
  2.7 1.2 %copy-done.2 = bf16[128,4096]{1,0:T(8,128)(2,1)S(1)} copy-done((bf16[128,4096]{1,0:T(8,128)(2,1)S(1)}, bf16[128,4096]{1,0:T(8,128)(2,1)}, u32[]{:S(2)}) %copy-start.2) | copy-done | bytes 1048600
  3.9 1.2 %copy-done.4 = bf16[128,4096]{1,0:T(8,128)(2,1)S(1)} copy-done((bf16[128,4096]{1,0:T(8,128)(2,1)S(1)}, bf16[128,4096]{1,0:T(8,128)(2,1)}, u32[]{:S(2)}) %copy-start.4) | copy-done | bytes 1048600
  5.1 1.2 %copy-done.6 = bf16[128,4096]{1,0:T(8,128)(2,1)S(1)} copy-done((bf16[128,4096]{1,0:T(8,128)(2,1)S(1)}, bf16[128,4096]{1,0:T(8,128)(2,1)}, u32[]{:S(2)}) %copy-start.6) | copy-done | bytes 1048600
  6.4 2.6 %shard_map.84 = bf16[16,272,128]{2,1,0:T(8,128)(2,1)S(1)} custom-call(s32[1]{0:T(128)S(6)} %sub.3.half_ref, bf16[128,32]{1,0:T(8,128)(2,1)S(1)} %copy.16.decay_ref, bf16[128,4096]{1,0:T(8,128)(2,1)S(1)} %copy-done, bf16[128,4096]{1,0:T(8,128)(2,1)S(1)} %copy-done.2, bf16[128,4096]{1,0:T(8,128)(2,1)S(1)} %copy-done.4, bf16[128,4096]{1,0:T(8,128)(2,1)S(1)} %copy-done.6), custom_call_target="tpu_custom_call" | custom-call | tf_op jit(solution)/shard_map/pallas_call | solution.py:305
  9.0 3.3 %collective-permute-start = (bf16[16,272,128]{2,1,0:T(8,128)(2,1)S(1)}, bf16[16,272,128]{2,1,0:T(8,128)(2,1)S(1)}, u32[]{:S(2)}, u32[]{:S(2)}) collective-permute-start(bf16[16,272,128]{2,1,0:T(8,128)(2,1)S(1)} %shard_map.84), channel_id=1, source_target_pairs={{0,1},{1,0},{2,3},{3,2},{4,5},{5,4},{6,7},{7,6},{8,9},{9,8},{10,11... | collective-permute-start | bytes 3342344 | tf_op jit(solution)/shard_map/ppermute | solution.py:332
  12.3 2.4 %collective-permute-done.other_ref = bf16[16,272,128]{2,1,0:T(8,128)(2,1)S(1)} collective-permute-done((bf16[16,272,128]{2,1,0:T(8,128)(2,1)S(1)}, bf16[16,272,128]{2,1,0:T(8,128)(2,1)S(1)}, u32[]{:S(2)}, u32[]{:S(2)}) %collective-permute-start) | collective-permute-done | bytes 1114144 | tf_op jit(solution)/shard_map/ppermute | solution.py:332
  14.7 1.0 %copy-done.13 = bf16[16,272,128]{2,1,0:T(8,128)(2,1)} copy-done((bf16[16,272,128]{2,1,0:T(8,128)(2,1)}, bf16[16,272,128]{2,1,0:T(8,128)(2,1)S(1)}, u32[]{:S(2)}) %copy-start.13) | copy-done | bytes 1114136
  15.7 4.8 %shard_map.85 = (bf16[16,272,128]{2,1,0:T(8,128)(2,1)S(1)}, bf16[32,144,128]{2,1,0:T(8,128)(2,1)}) custom-call(s32[1]{0:T(128)} %bitcast.half_ref, bf16[128,32]{1,0:T(8,128)(2,1)S(1)} %copy.16.decay_ref, bf16[128,4096]{1,0:T(8,128)(2,1)S(1)} %copy-done.1, bf16[128,4096]{1,0:T(8,128)(2,1)S(1)} %copy-done.3, bf16[128,4096]{1,0:T(8,128)(2,1)S(1)} %copy-done.5, ...), custom_call_target="tpu_custom_call" | custom-call | tf_op jit(solution)/shard_map/pallas_call | solution.py:305
  20.6 24.8 %all_to_all.10.pieces_ref = bf16[32,144,128]{2,1,0:T(8,128)(2,1)S(1)} all-to-all(bf16[32,144,128]{2,1,0:T(8,128)(2,1)} %get-tuple-element.11), channel_id=1, replica_groups=mesh['zh'=4,'zl'=2,'y'=4,'x'=4,'core'=2] {'zl','y','x'}, dimensions={0} | all-to-all | bytes 2359296 | tf_op jit(solution)/shard_map/all_to_all | solution.py:343
  45.3 0.4 shard_map.86
  45.7 1.0 %copy-done.9 = bf16[32,144,128]{2,1,0:T(8,128)(2,1)} copy-done((bf16[32,144,128]{2,1,0:T(8,128)(2,1)}, bf16[32,144,128]{2,1,0:T(8,128)(2,1)S(1)}, u32[]{:S(2)}) %copy-start.9) | copy-done | bytes 1179672
  46.8 5.1 %collective-permute-start.3 = (bf16[144,128]{1,0:T(8,128)(2,1)S(1)}, bf16[144,128]{1,0:T(8,128)(2,1)S(1)}, u32[]{:S(2)}, u32[]{:S(2)}) collective-permute-start(bf16[144,128]{1,0:T(8,128)(2,1)S(1)} %shard_map.86), channel_id=1, source_target_pairs={{0,192},{64,0},{128,64},{192,128},{1,193},{65,1},{129,65},{193,129... | collective-permute-start | bytes 110600 | tf_op jit(solution)/shard_map/ppermute | solution.py:351
  51.9 1.2 %collective-permute-start.2 = (bf16[144,128]{1,0:T(8,128)(2,1)S(1)}, bf16[144,128]{1,0:T(8,128)(2,1)S(1)}, u32[]{:S(2)}, u32[]{:S(2)}) collective-permute-start(bf16[144,128]{1,0:T(8,128)(2,1)S(1)} %shard_map.86), channel_id=1, source_target_pairs={{0,128},{64,192},{128,0},{192,64},{1,129},{65,193},{129,1},{193,65... | collective-permute-start | bytes 110600 | tf_op jit(solution)/shard_map/ppermute | solution.py:351
  53.1 2.1 %collective-permute-start.1 = (bf16[144,128]{1,0:T(8,128)(2,1)S(1)}, bf16[144,128]{1,0:T(8,128)(2,1)S(1)}, u32[]{:S(2)}, u32[]{:S(2)}) collective-permute-start(bf16[144,128]{1,0:T(8,128)(2,1)S(1)} %shard_map.86), channel_id=1, source_target_pairs={{0,64},{64,128},{128,192},{192,0},{1,65},{65,129},{129,193},{193,1... | collective-permute-start | bytes 110600 | tf_op jit(solution)/shard_map/ppermute | solution.py:351
  55.1 3.6 %collective-permute-done.2.two_ref = bf16[144,128]{1,0:T(8,128)(2,1)S(1)} collective-permute-done((bf16[144,128]{1,0:T(8,128)(2,1)S(1)}, bf16[144,128]{1,0:T(8,128)(2,1)S(1)}, u32[]{:S(2)}, u32[]{:S(2)}) %collective-permute-start.2) | collective-permute-done | bytes 36896 | tf_op jit(solution)/shard_map/ppermute | solution.py:351
  58.7 1.3 %copy-done.10 = bf16[32,144,128]{2,1,0:T(8,128)(2,1)S(1)} copy-done((bf16[32,144,128]{2,1,0:T(8,128)(2,1)S(1)}, bf16[32,144,128]{2,1,0:T(8,128)(2,1)}, u32[]{:S(2)}) %copy-start.10) | copy-done | bytes 1179672
  60.0 0.4 shard_map.87
  60.4 17.6 %all_to_all.11.pair_ref = bf16[32,128,128]{2,1,0:T(8,128)(2,1)S(1)} all-to-all(bf16[32,128,128]{2,1,0:T(8,128)(2,1)S(1)} %shard_map.87), channel_id=1, replica_groups=mesh['zh'=4,'zl'=2,'y'=4,'x'=4,'core'=2] {'zl','y','x'}, dimensions={0} | all-to-all | bytes 2097152 | tf_op jit(solution)/shard_map/all_to_all | solution.py:360
  78.0 0.6 shard_map.88
  78.7 4.6 %collective-permute-start.4 = (bf16[16,256,128]{2,1,0:T(8,128)(2,1)S(1)}, bf16[16,256,128]{2,1,0:T(8,128)(2,1)S(1)}, u32[]{:S(2)}, u32[]{:S(2)}) collective-permute-start(bf16[16,256,128]{2,1,0:T(8,128)(2,1)S(1)} %shard_map.88), channel_id=1, source_target_pairs={{0,1},{1,0},{2,3},{3,2},{4,5},{5,4},{6,7},{7,6},{8,9},{9,8},{10,11... | collective-permute-start | bytes 3145736 | tf_op jit(solution)/shard_map/ppermute | solution.py:367
  83.3 7.2 %shard_map.89 = (bf16[128,4096]{1,0:T(8,128)(2,1)}, bf16[128,4096]{1,0:T(8,128)(2,1)}, bf16[128,4096]{1,0:T(8,128)(2,1)}, bf16[128,4096]{1,0:T(8,128)(2,1)}) custom-call(s32[1]{0:T(128)} %bitcast.half_ref, bf16[128,32]{1,0:T(8,128)(2,1)S(1)} %copy.16.decay_ref, bf16[128,4096]{1,0:T(8,128)(2,1)S(1)} %copy-done.1, bf16[128,4096]{1,0:T(8,128)(2,1)S(1)} %copy-done.3, ...), custom_call_target="tpu_custom_call" | custom-call | tf_op jit(solution)/shard_map/pallas_call | solution.py:305
  90.5 6.3 %shard_map.90 = (bf16[128,4096]{1,0:T(8,128)(2,1)}, bf16[128,4096]{1,0:T(8,128)(2,1)}, bf16[128,4096]{1,0:T(8,128)(2,1)}, bf16[128,4096]{1,0:T(8,128)(2,1)}) custom-call(s32[1]{0:T(128)S(6)} %sub.3.half_ref, bf16[128,32]{1,0:T(8,128)(2,1)S(1)} %copy.16.decay_ref, ...), custom_call_target="tpu_custom_call", output_to_operand_aliasing={{0}: (7, {}), {1}: (8, {}), {2}: (9, {}), {3}: (10, {})} | custom-call | tf_op jit(solution)/shard_map/pallas_call | solution.py:305
  (24 shorter events, 0.0 us)
Async XLA Ops:
  1.4 1.2 %copy-start = (bf16[128,4096]{1,0:T(8,128)(2,1)S(1)}, bf16[128,4096]{1,0:T(8,128)(2,1)}, u32[]{:S(2)}) copy-start(bf16[128,4096]{1,0:T(8,128)(2,1)} %query_ref.7) | copy-start | bytes 3145732
  2.7 1.2 %copy-start.2 = (bf16[128,4096]{1,0:T(8,128)(2,1)S(1)}, bf16[128,4096]{1,0:T(8,128)(2,1)}, u32[]{:S(2)}) copy-start(bf16[128,4096]{1,0:T(8,128)(2,1)} %key_ref.7) | copy-start | bytes 3145732
  3.9 1.2 %copy-start.4 = (bf16[128,4096]{1,0:T(8,128)(2,1)S(1)}, bf16[128,4096]{1,0:T(8,128)(2,1)}, u32[]{:S(2)}) copy-start(bf16[128,4096]{1,0:T(8,128)(2,1)} %value_ref.7) | copy-start | bytes 3145732
  5.1 1.2 %copy-start.6 = (bf16[128,4096]{1,0:T(8,128)(2,1)S(1)}, bf16[128,4096]{1,0:T(8,128)(2,1)}, u32[]{:S(2)}) copy-start(bf16[128,4096]{1,0:T(8,128)(2,1)} %grad_ref.7) | copy-start | bytes 3145732
  6.4 9.4 %copy-start.1 = (bf16[128,4096]{1,0:T(8,128)(2,1)S(1)}, bf16[128,4096]{1,0:T(8,128)(2,1)}, u32[]{:S(2)}) copy-start(bf16[128,4096]{1,0:T(8,128)(2,1)} %query_ref.7) | copy-start | bytes 3145732
  6.4 9.4 %copy-start.3 = (bf16[128,4096]{1,0:T(8,128)(2,1)S(1)}, bf16[128,4096]{1,0:T(8,128)(2,1)}, u32[]{:S(2)}) copy-start(bf16[128,4096]{1,0:T(8,128)(2,1)} %key_ref.7) | copy-start | bytes 3145732
  6.4 9.4 %copy-start.5 = (bf16[128,4096]{1,0:T(8,128)(2,1)S(1)}, bf16[128,4096]{1,0:T(8,128)(2,1)}, u32[]{:S(2)}) copy-start(bf16[128,4096]{1,0:T(8,128)(2,1)} %value_ref.7) | copy-start | bytes 3145732
  6.4 9.4 %copy-start.7 = (bf16[128,4096]{1,0:T(8,128)(2,1)S(1)}, bf16[128,4096]{1,0:T(8,128)(2,1)}, u32[]{:S(2)}) copy-start(bf16[128,4096]{1,0:T(8,128)(2,1)} %grad_ref.7) | copy-start | bytes 3145732
  9.0 5.7 %collective-permute-start = (bf16[16,272,128]{2,1,0:T(8,128)(2,1)S(1)}, bf16[16,272,128]{2,1,0:T(8,128)(2,1)S(1)}, u32[]{:S(2)}, u32[]{:S(2)}) collective-permute-start(bf16[16,272,128]{2,1,0:T(8,128)(2,1)S(1)} %shard_map.84), channel_id=1, source_target_pairs={{0,1},{1,0},{2,3},{3,2},{4,5},{5,4},{6,7},{7,6},{8,9},{9,8},{10,11... | collective-permute-start | bytes 3342344 | tf_op jit(solution)/shard_map/ppermute | solution.py:332
  14.7 1.0 %copy-start.13 = (bf16[16,272,128]{2,1,0:T(8,128)(2,1)}, bf16[16,272,128]{2,1,0:T(8,128)(2,1)S(1)}, u32[]{:S(2)}) copy-start(bf16[16,272,128]{2,1,0:T(8,128)(2,1)S(1)} %collective-permute-done.other_ref) | copy-start | bytes 3342340
  20.5 24.8 %copy-start.11 = (bf16[16,272,128]{2,1,0:T(8,128)(2,1)}, bf16[16,272,128]{2,1,0:T(8,128)(2,1)S(1)}, u32[]{:S(2)}) copy-start(bf16[16,272,128]{2,1,0:T(8,128)(2,1)S(1)} %get-tuple-element.10.own_ref) | copy-start | bytes 3342340
  45.7 1.0 %copy-start.9 = (bf16[32,144,128]{2,1,0:T(8,128)(2,1)}, bf16[32,144,128]{2,1,0:T(8,128)(2,1)S(1)}, u32[]{:S(2)}) copy-start(bf16[32,144,128]{2,1,0:T(8,128)(2,1)S(1)} %all_to_all.10.pieces_ref) | copy-start | bytes 3538948
  46.8 8.4 %collective-permute-start.3 = (bf16[144,128]{1,0:T(8,128)(2,1)S(1)}, bf16[144,128]{1,0:T(8,128)(2,1)S(1)}, u32[]{:S(2)}, u32[]{:S(2)}) collective-permute-start(bf16[144,128]{1,0:T(8,128)(2,1)S(1)} %shard_map.86), channel_id=1, source_target_pairs={{0,192},{64,0},{128,64},{192,128},{1,193},{65,1},{129,65},{193,129... | collective-permute-start | bytes 110600 | tf_op jit(solution)/shard_map/ppermute | solution.py:351
  51.9 6.8 %collective-permute-start.2 = (bf16[144,128]{1,0:T(8,128)(2,1)S(1)}, bf16[144,128]{1,0:T(8,128)(2,1)S(1)}, u32[]{:S(2)}, u32[]{:S(2)}) collective-permute-start(bf16[144,128]{1,0:T(8,128)(2,1)S(1)} %shard_map.86), channel_id=1, source_target_pairs={{0,128},{64,192},{128,0},{192,64},{1,129},{65,193},{129,1},{193,65... | collective-permute-start | bytes 110600 | tf_op jit(solution)/shard_map/ppermute | solution.py:351
  53.1 5.7 %collective-permute-start.1 = (bf16[144,128]{1,0:T(8,128)(2,1)S(1)}, bf16[144,128]{1,0:T(8,128)(2,1)S(1)}, u32[]{:S(2)}, u32[]{:S(2)}) collective-permute-start(bf16[144,128]{1,0:T(8,128)(2,1)S(1)} %shard_map.86), channel_id=1, source_target_pairs={{0,64},{64,128},{128,192},{192,0},{1,65},{65,129},{129,193},{193,1... | collective-permute-start | bytes 110600 | tf_op jit(solution)/shard_map/ppermute | solution.py:351
  58.7 1.3 %copy-start.10 = (bf16[32,144,128]{2,1,0:T(8,128)(2,1)S(1)}, bf16[32,144,128]{2,1,0:T(8,128)(2,1)}, u32[]{:S(2)}) copy-start(bf16[32,144,128]{2,1,0:T(8,128)(2,1)} %copy-done.9) | copy-start | bytes 3538948
  60.4 17.6 %copy-start.12 = (bf16[16,272,128]{2,1,0:T(8,128)(2,1)S(1)}, bf16[16,272,128]{2,1,0:T(8,128)(2,1)}, u32[]{:S(2)}) copy-start(bf16[16,272,128]{2,1,0:T(8,128)(2,1)} %copy-done.11) | copy-start | bytes 3342340
  78.0 5.2 %copy-start.8 = (bf16[128,4096]{1,0:T(8,128)(2,1)S(1)}, bf16[128,4096]{1,0:T(8,128)(2,1)}, u32[]{:S(2)}) copy-start(bf16[128,4096]{1,0:T(8,128)(2,1)} %grad_ref.7) | copy-start | bytes 3145732
  78.7 11.8 %collective-permute-start.4 = (bf16[16,256,128]{2,1,0:T(8,128)(2,1)S(1)}, bf16[16,256,128]{2,1,0:T(8,128)(2,1)S(1)}, u32[]{:S(2)}, u32[]{:S(2)}) collective-permute-start(bf16[16,256,128]{2,1,0:T(8,128)(2,1)S(1)} %shard_map.88), channel_id=1, source_target_pairs={{0,1},{1,0},{2,3},{3,2},{4,5},{5,4},{6,7},{7,6},{8,9},{9,8},{10,11... | collective-permute-start | bytes 3145736 | tf_op jit(solution)/shard_map/ppermute | solution.py:367

commit v2 on v1

v2 whole, which is shorter than its diff:
```python
import jax
import jax.numpy as jnp
from jax import lax
from jax.experimental import pallas as pl
from jax.experimental.pallas import tpu as pltpu
from jax.sharding import Mesh, PartitionSpec as P

HEAD = 128
BLOCK = 128
HALF_HEADS = 16
STEPS = 4
PER_STEP = HALF_HEADS // STEPS
PART = HEAD // 2
TAIL = 8
SLAB = PER_STEP * HEAD
WIDTH = HALF_HEADS * HEAD
LOADS = 2
LOAD = WIDTH // LOADS
AXES = ("zh", "zl", "y", "x", "core")
GROUP = ("zl", "y", "x")

F32 = jnp.float32
BF16 = jnp.bfloat16
VMEM_LIMIT = 16 * 1024 * 1024


def dot(left, right, left_dim, right_dim):
    return lax.dot_general(
        left, right, (((left_dim,), (right_dim,)), ((), ())), preferred_element_type=F32
    )


def pack_decay(value):
    full = jnp.broadcast_to(value, (TAIL, HEAD))
    high = full.astype(BF16)
    rest = full - high.astype(F32)
    middle = rest.astype(BF16)
    low = (rest - middle.astype(F32)).astype(BF16)
    row = lax.broadcasted_iota(jnp.int32, (TAIL, HEAD), 0)
    chosen = jnp.where(
        row == 0, high.astype(F32), jnp.where(row == 1, middle.astype(F32), low.astype(F32))
    )
    return chosen.astype(BF16)


def unpack_decay(tile):
    rows = tile.astype(F32)
    return rows[0:1] + rows[1:2] + rows[2:3]


def lower_triangle():
    at = lax.broadcasted_iota(jnp.int32, (BLOCK, BLOCK), 0)
    before = lax.broadcasted_iota(jnp.int32, (BLOCK, BLOCK), 1)
    return at >= before


def half_decay(decay_ref, half):
    decay = decay_ref[...].astype(F32)
    return jnp.where(half == 0, decay[:HALF_HEADS], decay[HALF_HEADS:]).astype(BF16)


def column_scales(decay):
    cumul = dot(lower_triangle().astype(F32).astype(BF16), decay, 1, 1)
    finals = cumul[BLOCK - 1 : BLOCK, :]
    return jnp.exp(cumul), jnp.exp(finals - cumul), finals


def set_cumuls(decay, cols_ref, rows_ref):
    triangle = lower_triangle().astype(F32).astype(BF16)
    cumul = dot(triangle, decay, 1, 1)
    rows = dot(decay, triangle, 1, 1)
    for step in range(2 * STEPS):
        heads = slice(step * PER_STEP, (step + 1) * PER_STEP)
        cols_ref[step] = cumul[:, heads]
        rows_ref[step] = rows[heads]


def head_states(query, key, value, grad, fwd, bwd):
    scaled_key = (key.astype(F32) * bwd).astype(BF16)
    scaled_query = (query.astype(F32) * fwd).astype(BF16)
    return dot(scaled_key, value, 0, 0), dot(scaled_query, grad, 0, 0)


def write_states(spot, rows, fwd, bwd, finals, outs):
    cols = slice(spot * HEAD, (spot + 1) * HEAD)
    one = slice(spot, spot + 1)
    query, key, value, grad = (ref[:, cols] for ref in rows)
    kv, qd = head_states(query, key, value, grad, fwd[:, one], bwd[:, one])
    tail = pack_decay(finals[:, one])
    for out_ref in outs:
        out_ref[spot, 0:HEAD, :] = kv.astype(out_ref.dtype)
        out_ref[spot, HEAD : 2 * HEAD, :] = qd.astype(out_ref.dtype)
        out_ref[spot, 2 * HEAD :, :] = tail.astype(out_ref.dtype)


def sent_states(half_ref, decay_hbm, *refs):
    sources, out_ref, away, rows = refs[:4], refs[4], refs[5:9], refs[9:13]
    decay_ref, sems, away_sems, decay_sem = refs[13:]
    half = half_ref[0]

    def fetch(array, at):
        source = pl.multiple_of(half * WIDTH + at * LOAD, LOAD)
        return pltpu.make_async_copy(
            sources[array].at[:, pl.ds(source, LOAD)],
            rows[array].at[:, at * LOAD : (at + 1) * LOAD],
            sems.at[array, at],
        )

    def fetch_away(array):
        source = pl.multiple_of((1 - half) * WIDTH, WIDTH)
        return pltpu.make_async_copy(
            sources[array].at[:, pl.ds(source, WIDTH)], away[array], away_sems.at[array]
        )

    decay_copy = pltpu.make_async_copy(decay_hbm, decay_ref, decay_sem.at[0])
    decay_copy.start()
    for at in range(LOADS):
        for array in range(4):
            fetch(array, at).start()
    for array in range(4):
        fetch_away(array).start()
    decay_copy.wait()
    fwd, bwd, finals = column_scales(half_decay(decay_ref, half))
    for spot in range(HALF_HEADS):
        if spot % (HALF_HEADS // LOADS) == 0:
            for array in range(4):
                fetch(array, spot // (HALF_HEADS // LOADS)).wait()
        write_states(spot, rows, fwd, bwd, finals, (out_ref,))
    for array in range(4):
        fetch_away(array).wait()


def kept_states(half_ref, decay_ref, *refs):
    rows, outs = refs[:4], refs[4:]
    fwd, bwd, finals = column_scales(half_decay(decay_ref, half_ref[0]))
    for spot in range(HALF_HEADS):
        write_states(spot, rows, fwd, bwd, finals, outs)


def pair_states(half_ref, own_ref, other_ref, out_hbm, pair_ref, sems):
    first = half_ref[0] == 0
    chunk = 2 * HALF_HEADS // STEPS

    def send(step):
        spots = slice(step * chunk, (step + 1) * chunk)
        return pltpu.make_async_copy(pair_ref.at[spots], out_hbm.at[spots], sems.at[step])

    for head in range(HALF_HEADS):
        mine = unpack_decay(own_ref[head, 2 * HEAD :, :])
        theirs = unpack_decay(other_ref[head, 2 * HEAD :, :])
        decay_mine = jnp.exp(mine)
        decay_theirs = jnp.exp(theirs)
        unit = jnp.ones_like(mine)
        kv_scales = (jnp.where(first, decay_theirs, unit), jnp.where(first, unit, decay_mine))
        qd_scales = (jnp.where(first, unit, decay_theirs), jnp.where(first, decay_mine, unit))
        tail = pack_decay(mine + theirs)
        for part in range(2):
            piece = 2 * head + part
            for at, (scale_own, scale_other) in ((0, kv_scales), (1, qd_scales)):
                rows = slice(at * HEAD + part * PART, at * HEAD + (part + 1) * PART)
                joined = scale_own * own_ref[head, rows, :] + scale_other * other_ref[
                    head, rows, :
                ].astype(F32)
                pair_ref[piece, at * PART : (at + 1) * PART, :] = joined.astype(BF16)
            pair_ref[piece, 2 * PART :, :] = tail
        if (head + 1) % PER_STEP == 0:
            send(head // PER_STEP).start()
    for step in range(STEPS):
        send(step).wait()


def group_total(index_ref, pieces_ref, *outs):
    count = pieces_ref.shape[0]
    place = index_ref[0]
    zero = jnp.zeros((PART, HEAD), F32)

    def hop(at, carry):
        state, trail, total = carry
        back = count - 1 - at
        decay = unpack_decay(pieces_ref[at, 2 * PART :, :])
        decay_back = unpack_decay(pieces_ref[back, 2 * PART :, :])
        state = jnp.exp(decay) * state + pieces_ref[at, 0:PART, :].astype(F32)
        trail = jnp.exp(decay_back) * trail + pieces_ref[back, PART : 2 * PART, :].astype(F32)
        return state, trail, total + decay

    state, trail, total = lax.fori_loop(
        0, count, hop, (zero, zero, jnp.zeros((1, HEAD), F32)), unroll=8
    )
    tail = jnp.broadcast_to(total, (TAIL, HEAD))
    for distance, ref in enumerate(outs, 1):
        ref[0:PART, :] = jnp.where(place + distance <= len(outs), state, trail)
        ref[PART:, :] = tail


def group_entries(index_ref, pieces_ref, one_ref, two_ref, three_ref, out_ref):
    count = pieces_ref.shape[0]
    place = index_ref[0]
    state = jnp.zeros((PART, HEAD), F32)
    trail = jnp.zeros((PART, HEAD), F32)
    for distance, ref in ((3, three_ref), (2, two_ref), (1, one_ref)):
        longer = jnp.exp(ref[PART : PART + 1, :]) * state + ref[0:PART, :]
        state = jnp.where(place >= distance, longer, state)
    for distance, ref in ((1, one_ref), (2, two_ref), (3, three_ref)):
        longer = jnp.exp(ref[PART : PART + 1, :]) * trail + ref[0:PART, :]
        trail = jnp.where(place < distance, longer, trail)

    def hop(at, carry):
        state, trail = carry
        back = count - 1 - at
        out_ref[at, 0:PART, :] = state.astype(BF16)
        out_ref[back, PART : 2 * PART, :] = trail.astype(BF16)
        decay = unpack_decay(pieces_ref[at, 2 * PART :, :])
        decay_back = unpack_decay(pieces_ref[back, 2 * PART :, :])
        state = jnp.exp(decay) * state + pieces_ref[at, 0:PART, :].astype(F32)
        trail = jnp.exp(decay_back) * trail + pieces_ref[back, PART : 2 * PART, :].astype(F32)
        return state, trail

    lax.fori_loop(0, count, hop, (state, trail), unroll=8)


def other_entries(half_ref, own_ref, pair_ref, out_ref):
    first = half_ref[0] == 0
    for head in range(HALF_HEADS):
        decay = jnp.exp(unpack_decay(own_ref[head, 2 * HEAD :, :]))
        for part in range(2):
            rows = slice(part * PART, (part + 1) * PART)
            qd_rows = slice(HEAD + part * PART, HEAD + (part + 1) * PART)
            state = pair_ref[2 * head + part, 0:PART, :].astype(F32)
            trail = pair_ref[2 * head + part, PART : 2 * PART, :].astype(F32)
            later = decay * state + own_ref[head, rows, :].astype(F32)
            earlier = decay * trail + own_ref[head, qd_rows, :].astype(F32)
            out_ref[head, rows, :] = jnp.where(first, later, state).astype(BF16)
            out_ref[head, qd_rows, :] = jnp.where(first, trail, earlier).astype(BF16)


def inner_results(
    decay_ref, query_ref, key_ref, value_ref, grad_ref, att_ref, qg_ref, kg_ref, vg_ref, cols_ref, rows_ref
):
    step = pl.program_id(0)

    @pl.when(step == 0)
    def _():
        set_cumuls(decay_ref[...], cols_ref, rows_ref)

    lower = lower_triangle()
    for head in range(PER_STEP):
        cols = slice(head * HEAD, (head + 1) * HEAD)
        one = slice(head, head + 1)
        query, key, value, grad = (
            ref[:, cols] for ref in (query_ref, key_ref, value_ref, grad_ref)
        )
        spread = cols_ref[step][:, one] - rows_ref[step][one]
        weights = jnp.exp(jnp.where(lower, spread, -jnp.inf))
        probs = (dot(query, key, 1, 1) * weights).astype(BF16)
        grows = (dot(grad, value, 1, 1) * weights).astype(BF16)
        att_ref[:, cols] = dot(probs, value, 1, 0).astype(BF16)
        qg_ref[:, cols] = dot(grows, key, 1, 0).astype(BF16)
        kg_ref[:, cols] = dot(grows, query, 0, 0).astype(BF16)
        vg_ref[:, cols] = dot(probs, grad, 0, 0).astype(BF16)


def add_states(rows, inner, outs, spot, at, fwd, bwd, entering, trailing):
    cols = slice(spot * HEAD, (spot + 1) * HEAD)
    query, key, value, grad = (ref[:, cols] for ref in rows)
    terms = (
        fwd * dot(query, entering, 1, 0),
        fwd * dot(grad, entering, 1, 1),
        bwd * dot(value, trailing, 1, 1),
        bwd * dot(key, trailing, 1, 0),
    )
    for out, ref, term in zip(outs, inner, terms):
        out[:, at] = (ref[:, cols].astype(F32) + term).astype(BF16)


def result_copies(half, outs_hbm, outs, sems):
    def store(array, step):
        target = pl.multiple_of(half * WIDTH + step * SLAB, SLAB)
        return pltpu.make_async_copy(
            outs[array].at[:, step * SLAB : (step + 1) * SLAB],
            outs_hbm[array].at[:, pl.ds(target, SLAB)],
            sems.at[array, step],
        )

    return store


def own_results(half_ref, decay_ref, *refs):
    held, refs = refs[:8], refs[8:]
    pair_ref, other_ref = refs[:2]
    outs_hbm, refs = refs[2:6], refs[6:]
    away, refs = refs[:8], refs[8:]
    near, refs = refs[:8], refs[8:]
    outs, refs = refs[:4], refs[4:]
    near_sems, away_sems, out_sems = refs
    half = half_ref[0]
    first = half == 0

    def fetch(array, at):
        source = pl.multiple_of(half * WIDTH + at * LOAD, LOAD)
        return pltpu.make_async_copy(
            held[array].at[:, pl.ds(source, LOAD)],
            near[array].at[:, at * LOAD : (at + 1) * LOAD],
            near_sems.at[array, at],
        )

    def fetch_away(array):
        source = pl.multiple_of((1 - half) * WIDTH, WIDTH)
        return pltpu.make_async_copy(
            held[array].at[:, pl.ds(source, WIDTH)], away[array], away_sems.at[array]
        )

    store = result_copies(half, outs_hbm, outs, out_sems)
    for at in range(LOADS):
        for array in range(8):
            fetch(array, at).start()
    fwd, bwd, _ = column_scales(half_decay(decay_ref, half))
    for array in range(8):
        fetch_away(array).start()
    for spot in range(HALF_HEADS):
        if spot % (HALF_HEADS // LOADS) == 0:
            for array in range(8):
                fetch(array, spot // (HALF_HEADS // LOADS)).wait()
        step, head = divmod(spot, PER_STEP)
        one = slice(spot, spot + 1)
        decay = jnp.exp(unpack_decay(other_ref[spot, 2 * HEAD :, :]))
        left, right = pair_ref[2 * spot], pair_ref[2 * spot + 1]
        state = jnp.concatenate([left[0:PART], right[0:PART]], axis=0).astype(F32)
        trail = jnp.concatenate([left[PART:], right[PART:]], axis=0).astype(F32)
        later = decay * state + other_ref[spot, 0:HEAD, :].astype(F32)
        earlier = decay * trail + other_ref[spot, HEAD : 2 * HEAD, :].astype(F32)
        add_states(
            near[:4], near[4:], outs, spot, slice(spot * HEAD, (spot + 1) * HEAD),
            fwd[:, one], bwd[:, one],
            jnp.where(first, state, later).astype(BF16), jnp.where(first, earlier, trail).astype(BF16),
        )
        if head == PER_STEP - 1:
            for array in range(4):
                store(array, step).start()
    for array in range(8):
        fetch_away(array).wait()
    for step in range(STEPS):
        for array in range(4):
            store(array, step).wait()


def other_results(half_ref, decay_ref, *refs):
    away, entry_ref = refs[:8], refs[8]
    outs_hbm, refs = refs[13:17], refs[17:]
    outs, (out_sems,) = refs[:4], refs[4:]
    half = half_ref[0]
    store = result_copies(half, outs_hbm, outs, out_sems)
    fwd, bwd, _ = column_scales(half_decay(decay_ref, half))
    for spot in range(HALF_HEADS):
        step, head = divmod(spot, PER_STEP)
        one = slice(spot, spot + 1)
        entry = entry_ref[spot]
        add_states(
            away[:4], away[4:], outs, spot, slice(spot * HEAD, (spot + 1) * HEAD),
            fwd[:, one], bwd[:, one], entry[0:HEAD], entry[HEAD:],
        )
        if head == PER_STEP - 1:
            for array in range(4):
                store(array, step).start()
    for step in range(STEPS):
        for array in range(4):
            store(array, step).wait()


IN_VMEM = pl.BlockSpec(memory_space=pltpu.VMEM)
IN_HBM = pl.BlockSpec(memory_space=pl.ANY)
IN_SMEM = pl.BlockSpec(memory_space=pltpu.SMEM)
CUMULS = (
    pltpu.VMEM((2 * STEPS, BLOCK, PER_STEP), F32),
    pltpu.VMEM((2 * STEPS, PER_STEP, BLOCK), F32),
)


def once(kernel, operands, outputs, scratch=(), specs=None, out_specs=None, aliases=None):
    if specs is None:
        specs = [IN_SMEM if item.shape == (1,) else IN_VMEM for item in operands]
    return pl.pallas_call(
        kernel,
        out_shape=outputs,
        in_specs=specs,
        out_specs=out_specs or jax.tree.map(lambda _: IN_VMEM, outputs),
        scratch_shapes=list(scratch),
        input_output_aliases=aliases or {},
        compiler_params=pltpu.CompilerParams(vmem_limit_bytes=VMEM_LIMIT),
    )(*operands)


def in_hbm(item):
    return pltpu.with_memory_space_constraint(item, pltpu.HBM)


def shards(queries, key_rows, value_rows, out_grad, log_decay):
    core = lax.axis_index("core")
    mine = core.reshape(1).astype(jnp.int32)
    theirs = 1 - mine
    place = lax.axis_index("zh").reshape(1).astype(jnp.int32)
    rows = tuple(in_hbm(item) for item in (queries, key_rows, value_rows, out_grad))
    decay = log_decay.T
    decay_hbm = in_hbm(decay)
    state_rows = 2 * HEAD + TAIL
    piece_rows = 2 * PART + TAIL
    swap = [(0, 1), (1, 0)]
    states = (HALF_HEADS, state_rows, HEAD)
    pieces_shape = (2 * HALF_HEADS, piece_rows, HEAD)

    buffers = (pltpu.VMEM((BLOCK, WIDTH), BF16),)
    sent, *kept_rows = once(
        sent_states, (theirs, decay_hbm) + rows, [pltpu.VMEM(states, BF16)] + list(buffers * 4),
        buffers * 4
        + (
            pltpu.VMEM(decay.shape, BF16),
            pltpu.SemaphoreType.DMA((4, LOADS)),
            pltpu.SemaphoreType.DMA((4,)),
            pltpu.SemaphoreType.DMA((1,)),
        ),
        [IN_SMEM] + [IN_HBM] * 5,
    )
    other = lax.ppermute(sent, "core", swap)
    own, own_wide = once(
        kept_states, (mine, decay, *kept_rows), [pltpu.VMEM(states, BF16), pltpu.VMEM(states, F32)]
    )
    pairs = once(
        pair_states, (mine, own_wide, other), pltpu.HBM(pieces_shape, BF16),
        (pltpu.VMEM(pieces_shape, BF16), pltpu.SemaphoreType.DMA((STEPS,))),
        out_specs=IN_HBM,
    )
    pieces = lax.all_to_all(pairs, GROUP, split_axis=0, concat_axis=0, tiled=True)
    decay_later = lax.optimization_barrier((decay, pairs))[0]
    slab = pl.BlockSpec((BLOCK, SLAB), lambda step: (0, step))
    inner = pl.pallas_call(
        inner_results,
        out_shape=[pltpu.HBM(queries.shape, BF16)] * 4,
        grid_spec=pltpu.PrefetchScalarGridSpec(
            num_scalar_prefetch=0, grid=(2 * STEPS,),
            in_specs=[pl.BlockSpec(decay.shape, lambda step: (0, 0))] + [slab] * 4,
            out_specs=[slab] * 4, scratch_shapes=list(CUMULS),
        ),
        compiler_params=pltpu.CompilerParams(vmem_limit_bytes=VMEM_LIMIT),
    )(decay_later, *rows)
    pieces, inner = lax.optimization_barrier((pieces, inner))
    inner = tuple(in_hbm(item) for item in inner)
    size = lax.axis_size("zh")
    totals = once(group_total, (place, pieces), [pltpu.VMEM((PART + TAIL, HEAD), F32)] * (size - 1))
    moved = [
        lax.ppermute(total, "zh", [(at, (at + distance) % size) for at in range(size)])
        for distance, total in enumerate(totals, 1)
    ]
    entries = once(
        group_entries, (place, pieces, *moved), pltpu.VMEM((2 * HALF_HEADS, 2 * PART, HEAD), BF16)
    )
    pair_entries = lax.all_to_all(entries, GROUP, split_axis=0, concat_axis=0, tiled=True)
    leaving = once(
        other_entries, (mine, own, pair_entries), pltpu.VMEM((HALF_HEADS, 2 * HEAD, HEAD), BF16)
    )
    arrived = lax.ppermute(leaving, "core", swap)
    shapes = [pltpu.HBM(queries.shape, BF16)] * 4
    results = once(
        own_results, (mine, decay) + rows + inner + (pair_entries, other),
        shapes + list(buffers * 8),
        buffers * 12
        + (
            pltpu.SemaphoreType.DMA((8, LOADS)),
            pltpu.SemaphoreType.DMA((8,)),
            pltpu.SemaphoreType.DMA((4, STEPS)),
        ),
        [IN_SMEM, IN_VMEM] + [IN_HBM] * 8 + [IN_VMEM] * 2,
        [IN_HBM] * 4 + [IN_VMEM] * 8,
    )
    results = once(
        other_results, (theirs, decay) + tuple(results[4:]) + (arrived,) + tuple(results[:4]), shapes,
        buffers * 4 + (pltpu.SemaphoreType.DMA((4, STEPS)),),
        [IN_SMEM] + [IN_VMEM] * 10 + [IN_HBM] * 4, [IN_HBM] * 4,
        {11: 0, 12: 1, 13: 2, 14: 3},
    )
    return tuple(results)


def solution(mesh):
    chain, inner = mesh.devices.shape
    grid = Mesh(mesh.devices.reshape(chain // 2, 2, 4, 4, inner // 16), AXES)
    spec = P(AXES, None)
    return jax.shard_map(
        shards, mesh=grid, in_specs=(spec,) * 5, out_specs=(spec,) * 4, check_vma=False
    )
```

time: 97.4 us -> 78.7 us (0.81)
  blocking collectives: 42.4 us -> 19.3 us
  local copies, waits for them, and re-layouts: 9.04 us -> 0.01 us
  starting transfers between devices: 16.3 us -> 24.3 us
  Pallas kernels: 22.4 us -> 27.4 us
    all_to_all x1 -> x0, blocking collectives: 24.8 us -> none  [shards(): lax.all_to_all(pairs, GROUP, split_axis=0, concat_axis=0, tiled=True)]
    unnamed x29 -> x2, local copies, waits for them, and re-layouts: 9.04 us -> 0.01 us
    all_to_all x0 -> x1, starting transfers between devices: none -> 6.67 us  [shards(): lax.all_to_all(pairs, GROUP, split_axis=0, concat_axis=0, tiled=True)]
    pallas_call x7 -> x9, Pallas kernels: 22.4 us -> 27.4 us  [the longest x8 16.1 us: once(): pl.pallas_call(kernel, out_shape=outputs, in_specs=specs, out_specs=out_s...]
    all_to_all x0 -> x1, waiting for transfers between devices: none -> 4.58 us  [shards(): lax.all_to_all(pairs, GROUP, split_axis=0, concat_axis=0, tiled=True)]
    ppermute x3, waiting for transfers between devices: 3.56 us -> 1.58 us  [shards(): lax.ppermute(total, 'zh', [(at, (at + distance) % size) for at in range(s...]
    ppermute x1, waiting for transfers between devices: 2.38 us -> 0.46 us  [shards(): other = lax.ppermute(sent, 'core', swap)]
    all_to_all x1, blocking collectives: 17.6 us -> 19.3 us  [shards(): lax.all_to_all(entries, GROUP, split_axis=0, concat_axis=0, tiled=True)]
  transfers between devices with their start and end apart: 5 -> 6, of which waited for: 2 -> 4; matrix products, arithmetic and copies ran while one was open for 0% -> 0% of each run, Pallas kernels for 7% -> 24%
where the time goes in v2:
time: 78.7 us; the launch traced here: 78.3 us
  Pallas kernels  27.4 us (35%)
  starting transfers between devices  24.3 us (31%)
  blocking collectives  19.3 us (25%)
  waiting for transfers between devices  6.62 us (8%)
    all_to_all x1, blocking collectives, shards(): lax.all_to_all(entries, GROUP, split_axis=0, concat_axis=0, tiled=True)  19.3 us
    pallas_call x8, Pallas kernels, once(): pl.pallas_call(kernel, out_shape=outputs, in_specs=specs, out_specs=out_s...  16.1 us
    pallas_call x1, Pallas kernels, shards(): pl.pallas_call(inner_results, out_shape=[pltpu.HBM(queries.shape, BF16)]...  11.2 us
    ppermute x3, starting transfers between devices, shards(): lax.ppermute(total, 'zh', [(at, (at + distance) % size) for at in range(s...  9.67 us
    all_to_all x1, starting transfers between devices, shards(): lax.all_to_all(pairs, GROUP, split_axis=0, concat_axis=0, tiled=True)  6.67 us
    ppermute x1, starting transfers between devices, shards(): arrived = lax.ppermute(leaving, 'core', swap)  4.6 us
    all_to_all x1, waiting for transfers between devices, shards(): lax.all_to_all(pairs, GROUP, split_axis=0, concat_axis=0, tiled=True)  4.58 us
    ppermute x1, starting transfers between devices, shards(): other = lax.ppermute(sent, 'core', swap)  3.35 us
  transfers between devices with their start and end apart: 6, of which 4 were waited for; matrix products, arithmetic and copies ran while one was open for 0% of the time, Pallas kernels for 24%

profile of v2, /device:TPU:1, one launch (start us, length us, event | category | flops | bytes accessed | tf_op | source)
XLA Modules:
  0.0 78.3 jit_solution(4558618122723056306)
XLA Ops:
  0.6 0.0 copy-start
  0.6 4.1 %shard_map.84 = (bf16[16,264,128]{2,1,0:T(8,128)(2,1)S(1)}, bf16[128,2048]{1,0:T(8,128)(2,1)S(1)}, bf16[128,2048]{1,0:T(8,128)(2,1)S(1)}, bf16[128,2048]{1,0:T(8,128)(2,1)S(1)}, bf16[128,2048]{1,0:T(8,128)(2,1)S(1)}) custom-call(s32[1]{0:T(128)S(6)} %sub.3.half_ref, bf16[32,128]{1,0:T(8,128)(2,1)} %bitcast.3, bf16[128,4096]{1,0:T(8,128)(2,1)} %refs_0_.3, ...), custom_call_target="tpu_custom_call" | custom-call | tf_op jit(solution)/shard_map/pallas_call | solution.py:381
  4.7 3.3 %collective-permute-start = (bf16[16,264,128]{2,1,0:T(8,128)(2,1)S(1)}, bf16[16,264,128]{2,1,0:T(8,128)(2,1)S(1)}, u32[]{:S(2)}, u32[]{:S(2)}) collective-permute-start(bf16[16,264,128]{2,1,0:T(8,128)(2,1)S(1)} %get-tuple-element.41), channel_id=1, source_target_pairs={{0,1},{1,0},{2,3},{3,2},{4,5},{5,4},{6,7},{7,6},{8,9},{9,8},{10,11... | collective-permute-start | bytes 3244040 | tf_op jit(solution)/shard_map/ppermute | solution.py:422
  8.1 0.0 copy-done
  8.1 1.9 %shard_map.85 = (bf16[16,264,128]{2,1,0:T(8,128)(2,1)S(1)}, f32[16,264,128]{2,1,0:T(8,128)S(1)}) custom-call(s32[1]{0:T(128)} %bitcast.half_ref, bf16[32,128]{1,0:T(8,128)(2,1)S(1)} %bitcast.4, bf16[128,2048]{1,0:T(8,128)(2,1)S(1)} %get-tuple-element.36.refs_0_, bf16[128,2048]{1,0:T(8,128)(2,1)S(1)} %get-tuple-element.37.refs_1_, ...), custom_call_target="tpu_custom_call" | custom-call | tf_op jit(solution)/shard_map/pallas_call | solution.py:381
  10.0 0.5 collective-permute-done.other_ref.refs_9_
  10.4 1.2 %shard_map.86 = bf16[32,136,128]{2,1,0:T(8,128)(2,1)} custom-call(s32[1]{0:T(128)} %bitcast.half_ref, f32[16,264,128]{2,1,0:T(8,128)S(1)} %get-tuple-element.40.own_ref, bf16[16,264,128]{2,1,0:T(8,128)(2,1)S(1)} %collective-permute-done.other_ref.refs_9_), custom_call_target="tpu_custom_call" | custom-call | tf_op jit(solution)/shard_map/pallas_call | solution.py:381
  11.6 6.7 %all-to-all-start = ((bf16[32,136,128]{2,1,0:T(8,128)(2,1)}), bf16[32,136,128]{2,1,0:T(8,128)(2,1)S(1)}, u32[]{:S(2)}, u32[]{:S(2)}) async-start(bf16[32,136,128]{2,1,0:T(8,128)(2,1)} %shard_map.86), calls=%async_computation | async-start | bytes 2228224 | tf_op jit(solution)/shard_map/all_to_all | solution.py:431
  18.3 11.2 %shard_map.87 = (bf16[128,4096]{1,0:T(8,128)(2,1)}, bf16[128,4096]{1,0:T(8,128)(2,1)}, bf16[128,4096]{1,0:T(8,128)(2,1)}, bf16[128,4096]{1,0:T(8,128)(2,1)}) custom-call(bf16[32,128]{1,0:T(8,128)(2,1)S(1)} %bitcast.5, bf16[128,4096]{1,0:T(8,128)(2,1)} %refs_0_.3, bf16[128,4096]{1,0:T(8,128)(2,1)} %refs_1_.3, bf16[128,4096]{1,0:T(8,128)(2,1)} %refs_2_.3, ...), custom_call_target="tpu_custom_call" | custom-call | tf_op jit(solution)/shard_map/pallas_call | solution.py:434
  29.5 4.6 %all-to-all-done.pieces_ref = bf16[32,136,128]{2,1,0:T(8,128)(2,1)S(1)} async-done(((bf16[32,136,128]{2,1,0:T(8,128)(2,1)}), bf16[32,136,128]{2,1,0:T(8,128)(2,1)S(1)}, u32[]{:S(2)}, u32[]{:S(2)}) %all-to-all-start) | async-done | bytes 1114144 | tf_op jit(solution)/shard_map/all_to_all | solution.py:431
  34.1 0.3 shard_map.88
  34.4 3.1 %collective-permute-start.1 = (f32[72,128]{1,0:T(8,128)S(1)}, f32[72,128]{1,0:T(8,128)S(1)}, u32[]{:S(2)}, u32[]{:S(2)}) collective-permute-start(f32[72,128]{1,0:T(8,128)S(1)} %get-tuple-element.52), channel_id=1, source_target_pairs={{0,64},{64,128},{128,192},{192,0},{1,65},{65,129},{129,193},{193,1... | collective-permute-start | bytes 110600 | tf_op jit(solution)/shard_map/ppermute | solution.py:449
  37.5 4.2 %collective-permute-start.2 = (f32[72,128]{1,0:T(8,128)S(1)}, f32[72,128]{1,0:T(8,128)S(1)}, u32[]{:S(2)}, u32[]{:S(2)}) collective-permute-start(f32[72,128]{1,0:T(8,128)S(1)} %get-tuple-element.53), channel_id=1, source_target_pairs={{0,128},{64,192},{128,0},{192,64},{1,129},{65,193},{129,1},{193,65... | collective-permute-start | bytes 110600 | tf_op jit(solution)/shard_map/ppermute | solution.py:449
  41.7 2.4 %collective-permute-start.3 = (f32[72,128]{1,0:T(8,128)S(1)}, f32[72,128]{1,0:T(8,128)S(1)}, u32[]{:S(2)}, u32[]{:S(2)}) collective-permute-start(f32[72,128]{1,0:T(8,128)S(1)} %get-tuple-element.54), channel_id=1, source_target_pairs={{0,192},{64,0},{128,64},{192,128},{1,193},{65,1},{129,65},{193,129... | collective-permute-start | bytes 110600 | tf_op jit(solution)/shard_map/ppermute | solution.py:449
  44.1 0.0 collective-permute-done.1.one_ref
  44.1 0.2 collective-permute-done.2.two_ref
  44.3 1.4 %collective-permute-done.3.three_ref = f32[72,128]{1,0:T(8,128)S(1)} collective-permute-done((f32[72,128]{1,0:T(8,128)S(1)}, f32[72,128]{1,0:T(8,128)S(1)}, u32[]{:S(2)}, u32[]{:S(2)}) %collective-permute-start.3) | collective-permute-done | bytes 36896 | tf_op jit(solution)/shard_map/ppermute | solution.py:449
  45.7 0.4 shard_map.89
  46.1 19.3 %all_to_all.10.refs_8_.pair_ref = bf16[32,128,128]{2,1,0:T(8,128)(2,1)S(1)} all-to-all(bf16[32,128,128]{2,1,0:T(8,128)(2,1)S(1)} %shard_map.89), channel_id=1, replica_groups=mesh['zh'=4,'zl'=2,'y'=4,'x'=4,'core'=2] {'zl','y','x'}, dimensions={0} | all-to-all | bytes 2097152 | tf_op jit(solution)/shard_map/all_to_all | solution.py:455
  65.4 0.6 shard_map.91
  65.9 4.6 %collective-permute-start.4 = (bf16[16,256,128]{2,1,0:T(8,128)(2,1)S(1)}, bf16[16,256,128]{2,1,0:T(8,128)(2,1)S(1)}, u32[]{:S(2)}, u32[]{:S(2)}) collective-permute-start(bf16[16,256,128]{2,1,0:T(8,128)(2,1)S(1)} %shard_map.91), channel_id=1, source_target_pairs={{0,1},{1,0},{2,3},{3,2},{4,5},{5,4},{6,7},{7,6},{8,9},{9,8},{10,11... | collective-permute-start | bytes 3145736 | tf_op jit(solution)/shard_map/ppermute | solution.py:459
  70.5 5.5 %shard_map.90 = (bf16[128,4096]{1,0:T(8,128)(2,1)}, bf16[128,4096]{1,0:T(8,128)(2,1)}, bf16[128,4096]{1,0:T(8,128)(2,1)}, bf16[128,4096]{1,0:T(8,128)(2,1)}, bf1...) custom-call(s32[1]{0:T(128)} %bitcast.half_ref, ...), custom_call_target="tpu_custom_call" | custom-call | tf_op jit(solution)/shard_map/pallas_call | solution.py:381
  76.0 0.0 collective-permute-done.4.refs_8_
  76.0 2.3 %shard_map.92 = (bf16[128,4096]{1,0:T(8,128)(2,1)}, bf16[128,4096]{1,0:T(8,128)(2,1)}, bf16[128,4096]{1,0:T(8,128)(2,1)}, bf16[128,4096]{1,0:T(8,128)(2,1)}) custom-call(s32[1]{0:T(128)S(6)} %sub.3.half_ref, bf16[32,128]{1,0:T(8,128)(2,1)S(1)} %bitcast.7, ...), custom_call_target="tpu_custom_call", output_to_operand_aliasing={{0}: (11, {}), {1}: (12, {}), {2}: (13, {}), {3}: (14, {})} | custom-call | tf_op jit(solution)/shard_map/pallas_call | solution.py:381
Async XLA Ops:
  0.6 7.5 %copy-start = (bf16[128,32]{0,1:T(8,128)(2,1)S(1)}, bf16[128,32]{0,1:T(8,128)(2,1)}, u32[]{:S(2)}) copy-start(bf16[128,32]{0,1:T(8,128)(2,1)} %param.9) | copy-start | bytes 24580
  4.7 5.7 %collective-permute-start = (bf16[16,264,128]{2,1,0:T(8,128)(2,1)S(1)}, bf16[16,264,128]{2,1,0:T(8,128)(2,1)S(1)}, u32[]{:S(2)}, u32[]{:S(2)}) collective-permute-start(bf16[16,264,128]{2,1,0:T(8,128)(2,1)S(1)} %get-tuple-element.41), channel_id=1, source_target_pairs={{0,1},{1,0},{2,3},{3,2},{4,5},{5,4},{6,7},{7,6},{8,9},{9,8},{10,11... | collective-permute-start | bytes 3244040 | tf_op jit(solution)/shard_map/ppermute | solution.py:422
  11.6 22.5 %all-to-all-start = ((bf16[32,136,128]{2,1,0:T(8,128)(2,1)}), bf16[32,136,128]{2,1,0:T(8,128)(2,1)S(1)}, u32[]{:S(2)}, u32[]{:S(2)}) async-start(bf16[32,136,128]{2,1,0:T(8,128)(2,1)} %shard_map.86), calls=%async_computation | async-start | bytes 2228224 | tf_op jit(solution)/shard_map/all_to_all | solution.py:431
  34.4 9.7 %collective-permute-start.1 = (f32[72,128]{1,0:T(8,128)S(1)}, f32[72,128]{1,0:T(8,128)S(1)}, u32[]{:S(2)}, u32[]{:S(2)}) collective-permute-start(f32[72,128]{1,0:T(8,128)S(1)} %get-tuple-element.52), channel_id=1, source_target_pairs={{0,64},{64,128},{128,192},{192,0},{1,65},{65,129},{129,193},{193,1... | collective-permute-start | bytes 110600 | tf_op jit(solution)/shard_map/ppermute | solution.py:449
  37.5 6.8 %collective-permute-start.2 = (f32[72,128]{1,0:T(8,128)S(1)}, f32[72,128]{1,0:T(8,128)S(1)}, u32[]{:S(2)}, u32[]{:S(2)}) collective-permute-start(f32[72,128]{1,0:T(8,128)S(1)} %get-tuple-element.53), channel_id=1, source_target_pairs={{0,128},{64,192},{128,0},{192,64},{1,129},{65,193},{129,1},{193,65... | collective-permute-start | bytes 110600 | tf_op jit(solution)/shard_map/ppermute | solution.py:449
  41.7 4.0 %collective-permute-start.3 = (f32[72,128]{1,0:T(8,128)S(1)}, f32[72,128]{1,0:T(8,128)S(1)}, u32[]{:S(2)}, u32[]{:S(2)}) collective-permute-start(f32[72,128]{1,0:T(8,128)S(1)} %get-tuple-element.54), channel_id=1, source_target_pairs={{0,192},{64,0},{128,64},{192,128},{1,193},{65,1},{129,65},{193,129... | collective-permute-start | bytes 110600 | tf_op jit(solution)/shard_map/ppermute | solution.py:449
  65.9 10.1 %collective-permute-start.4 = (bf16[16,256,128]{2,1,0:T(8,128)(2,1)S(1)}, bf16[16,256,128]{2,1,0:T(8,128)(2,1)S(1)}, u32[]{:S(2)}, u32[]{:S(2)}) collective-permute-start(bf16[16,256,128]{2,1,0:T(8,128)(2,1)S(1)} %shard_map.91), channel_id=1, source_target_pairs={{0,1},{1,0},{2,3},{3,2},{4,5},{5,4},{6,7},{7,6},{8,9},{9,8},{10,11... | collective-permute-start | bytes 3145736 | tf_op jit(solution)/shard_map/ppermute | solution.py:459

commit v3 on v2

--- a/solution.py
+++ b/solution.py
@@ -16,6 +16,8 @@
 WIDTH = HALF_HEADS * HEAD
 LOADS = 2
 LOAD = WIDTH // LOADS
+HELD = 2
+DISTANCES = (2, 1, 3)
 AXES = ("zh", "zl", "y", "x", "core")
 GROUP = ("zl", "y", "x")
 
@@ -114,17 +116,19 @@
 
     decay_copy = pltpu.make_async_copy(decay_hbm, decay_ref, decay_sem.at[0])
     decay_copy.start()
-    for at in range(LOADS):
-        for array in range(4):
-            fetch(array, at).start()
     for array in range(4):
-        fetch_away(array).start()
+        fetch(array, 0).start()
     decay_copy.wait()
     fwd, bwd, finals = column_scales(half_decay(decay_ref, half))
+    for array in range(4):
+        fetch(array, 1).start()
     for spot in range(HALF_HEADS):
         if spot % (HALF_HEADS // LOADS) == 0:
             for array in range(4):
                 fetch(array, spot // (HALF_HEADS // LOADS)).wait()
+        if spot == PER_STEP:
+            for array in range(4):
+                fetch_away(array).start()
         write_states(spot, rows, fwd, bwd, finals, (out_ref,))
     for array in range(4):
         fetch_away(array).wait()
@@ -137,7 +141,9 @@
         write_states(spot, rows, fwd, bwd, finals, outs)
 
 
-def pair_states(half_ref, own_ref, other_ref, out_hbm, pair_ref, sems):
+def pair_states(half_ref, own_ref, other_ref, out_hbm, mine_ref, their_ref, pair_ref, sems):
+    kept_from = pl.multiple_of(half_ref[0] * HEAD, HEAD)
+    their_from = pl.multiple_of((1 - half_ref[0]) * HEAD, HEAD)
     first = half_ref[0] == 0
     chunk = 2 * HALF_HEADS // STEPS
 
@@ -165,6 +171,11 @@
             pair_ref[piece, 2 * PART :, :] = tail
         if (head + 1) % PER_STEP == 0:
             send(head // PER_STEP).start()
+    for head in range(HALF_HEADS):
+        mine_ref[head, 0:HEAD, :] = own_ref[head, pl.ds(kept_from, HEAD), :].astype(BF16)
+        mine_ref[head, HEAD:, :] = own_ref[head, 2 * HEAD :, :].astype(BF16)
+        their_ref[head, 0:HEAD, :] = other_ref[head, pl.ds(their_from, HEAD), :]
+        their_ref[head, HEAD:, :] = other_ref[head, 2 * HEAD :, :]
     for step in range(STEPS):
         send(step).wait()
 
@@ -187,12 +198,12 @@
         0, count, hop, (zero, zero, jnp.zeros((1, HEAD), F32)), unroll=8
     )
     tail = jnp.broadcast_to(total, (TAIL, HEAD))
-    for distance, ref in enumerate(outs, 1):
+    for distance, ref in zip(DISTANCES, outs):
         ref[0:PART, :] = jnp.where(place + distance <= len(outs), state, trail)
         ref[PART:, :] = tail
 
 
-def group_entries(index_ref, pieces_ref, one_ref, two_ref, three_ref, out_ref):
+def group_entries(index_ref, pieces_ref, two_ref, one_ref, three_ref, out_ref):
     count = pieces_ref.shape[0]
     place = index_ref[0]
     state = jnp.zeros((PART, HEAD), F32)
@@ -218,19 +229,23 @@
     lax.fori_loop(0, count, hop, (state, trail), unroll=8)
 
 
-def other_entries(half_ref, own_ref, pair_ref, out_ref):
-    first = half_ref[0] == 0
+def write_entries(changed, states_ref, pair_ref, out_ref):
+    step_from = pl.multiple_of(changed * PART, PART)
+    same_from = pl.multiple_of((1 - changed) * PART, PART)
     for head in range(HALF_HEADS):
-        decay = jnp.exp(unpack_decay(own_ref[head, 2 * HEAD :, :]))
+        decay = jnp.exp(unpack_decay(states_ref[head, HEAD:, :]))
         for part in range(2):
-            rows = slice(part * PART, (part + 1) * PART)
-            qd_rows = slice(HEAD + part * PART, HEAD + (part + 1) * PART)
-            state = pair_ref[2 * head + part, 0:PART, :].astype(F32)
-            trail = pair_ref[2 * head + part, PART : 2 * PART, :].astype(F32)
-            later = decay * state + own_ref[head, rows, :].astype(F32)
-            earlier = decay * trail + own_ref[head, qd_rows, :].astype(F32)
-            out_ref[head, rows, :] = jnp.where(first, later, state).astype(BF16)
-            out_ref[head, qd_rows, :] = jnp.where(first, trail, earlier).astype(BF16)
+            lines = slice(part * PART, (part + 1) * PART)
+            carried = pair_ref[2 * head + part, pl.ds(step_from, PART), :].astype(F32)
+            joined = decay * carried + states_ref[head, lines, :].astype(F32)
+            step_to = pl.multiple_of(changed * HEAD + part * PART, PART)
+            same_to = pl.multiple_of((1 - changed) * HEAD + part * PART, PART)
+            out_ref[head, pl.ds(step_to, PART), :] = joined.astype(BF16)
+            out_ref[head, pl.ds(same_to, PART), :] = pair_ref[2 * head + part, pl.ds(same_from, PART), :]
+
+
+def other_entries(half_ref, mine_ref, pair_ref, out_ref):
+    write_entries(half_ref[0], mine_ref, pair_ref, out_ref)
 
 
 def inner_results(
@@ -286,14 +301,13 @@
 
 def own_results(half_ref, decay_ref, *refs):
     held, refs = refs[:8], refs[8:]
-    pair_ref, other_ref = refs[:2]
-    outs_hbm, refs = refs[2:6], refs[6:]
+    near, (pair_ref, their_ref), refs = refs[:HELD], refs[HELD : HELD + 2], refs[HELD + 2 :]
+    outs_hbm, refs = refs[:4], refs[4:]
     away, refs = refs[:8], refs[8:]
-    near, refs = refs[:8], refs[8:]
+    near, refs = near + refs[: 8 - HELD], refs[8 - HELD :]
     outs, refs = refs[:4], refs[4:]
-    near_sems, away_sems, out_sems = refs
+    entry_ref, near_sems, away_sems, out_sems = refs
     half = half_ref[0]
-    first = half == 0
 
     def fetch(array, at):
         source = pl.multiple_of(half * WIDTH + at * LOAD, LOAD)
@@ -310,28 +324,25 @@
         )
 
     store = result_copies(half, outs_hbm, outs, out_sems)
-    for at in range(LOADS):
-        for array in range(8):
-            fetch(array, at).start()
+    for array in range(HELD, 8):
+        fetch(array, 0).start()
     fwd, bwd, _ = column_scales(half_decay(decay_ref, half))
-    for array in range(8):
-        fetch_away(array).start()
+    write_entries(1 - half, their_ref, pair_ref, entry_ref)
+    for array in range(HELD, 8):
+        fetch(array, 1).start()
     for spot in range(HALF_HEADS):
         if spot % (HALF_HEADS // LOADS) == 0:
+            for array in range(HELD, 8):
+                fetch(array, spot // (HALF_HEADS // LOADS)).wait()
+        if spot == PER_STEP:
             for array in range(8):
-                fetch(array, spot // (HALF_HEADS // LOADS)).wait()
+                fetch_away(array).start()
         step, head = divmod(spot, PER_STEP)
         one = slice(spot, spot + 1)
-        decay = jnp.exp(unpack_decay(other_ref[spot, 2 * HEAD :, :]))
-        left, right = pair_ref[2 * spot], pair_ref[2 * spot + 1]
-        state = jnp.concatenate([left[0:PART], right[0:PART]], axis=0).astype(F32)
-        trail = jnp.concatenate([left[PART:], right[PART:]], axis=0).astype(F32)
-        later = decay * state + other_ref[spot, 0:HEAD, :].astype(F32)
-        earlier = decay * trail + other_ref[spot, HEAD : 2 * HEAD, :].astype(F32)
+        entry = entry_ref[spot]
         add_states(
             near[:4], near[4:], outs, spot, slice(spot * HEAD, (spot + 1) * HEAD),
-            fwd[:, one], bwd[:, one],
-            jnp.where(first, state, later).astype(BF16), jnp.where(first, earlier, trail).astype(BF16),
+            fwd[:, one], bwd[:, one], entry[0:HEAD], entry[HEAD:],
         )
         if head == PER_STEP - 1:
             for array in range(4):
@@ -420,13 +431,12 @@
         [IN_SMEM] + [IN_HBM] * 5,
     )
     other = lax.ppermute(sent, "core", swap)
-    own, own_wide = once(
-        kept_states, (mine, decay, *kept_rows), [pltpu.VMEM(states, BF16), pltpu.VMEM(states, F32)]
-    )
-    pairs = once(
-        pair_states, (mine, own_wide, other), pltpu.HBM(pieces_shape, BF16),
+    (own,) = once(kept_states, (mine, decay, *kept_rows), [pltpu.VMEM(states, F32)])
+    part_states = pltpu.VMEM((HALF_HEADS, HEAD + TAIL, HEAD), BF16)
+    pairs, own_part, other_part = once(
+        pair_states, (mine, own, other), [pltpu.HBM(pieces_shape, BF16), part_states, part_states],
         (pltpu.VMEM(pieces_shape, BF16), pltpu.SemaphoreType.DMA((STEPS,))),
-        out_specs=IN_HBM,
+        out_specs=[IN_HBM, IN_VMEM, IN_VMEM],
     )
     pieces = lax.all_to_all(pairs, GROUP, split_axis=0, concat_axis=0, tiled=True)
     decay_later = lax.optimization_barrier((decay, pairs))[0]
@@ -447,27 +457,28 @@
     totals = once(group_total, (place, pieces), [pltpu.VMEM((PART + TAIL, HEAD), F32)] * (size - 1))
     moved = [
         lax.ppermute(total, "zh", [(at, (at + distance) % size) for at in range(size)])
-        for distance, total in enumerate(totals, 1)
+        for distance, total in zip(DISTANCES, totals)
     ]
     entries = once(
         group_entries, (place, pieces, *moved), pltpu.VMEM((2 * HALF_HEADS, 2 * PART, HEAD), BF16)
     )
     pair_entries = lax.all_to_all(entries, GROUP, split_axis=0, concat_axis=0, tiled=True)
     leaving = once(
-        other_entries, (mine, own, pair_entries), pltpu.VMEM((HALF_HEADS, 2 * HEAD, HEAD), BF16)
+        other_entries, (mine, own_part, pair_entries), pltpu.VMEM((HALF_HEADS, 2 * HEAD, HEAD), BF16)
     )
     arrived = lax.ppermute(leaving, "core", swap)
     shapes = [pltpu.HBM(queries.shape, BF16)] * 4
     results = once(
-        own_results, (mine, decay) + rows + inner + (pair_entries, other),
+        own_results, (mine, decay) + rows + inner + tuple(kept_rows[:HELD]) + (pair_entries, other_part),
         shapes + list(buffers * 8),
-        buffers * 12
+        buffers * (12 - HELD)
         + (
+            pltpu.VMEM((HALF_HEADS, 2 * HEAD, HEAD), BF16),
             pltpu.SemaphoreType.DMA((8, LOADS)),
             pltpu.SemaphoreType.DMA((8,)),
             pltpu.SemaphoreType.DMA((4, STEPS)),
         ),
-        [IN_SMEM, IN_VMEM] + [IN_HBM] * 8 + [IN_VMEM] * 2,
+        [IN_SMEM, IN_VMEM] + [IN_HBM] * 8 + [IN_VMEM] * (2 + HELD),
         [IN_HBM] * 4 + [IN_VMEM] * 8,
     )
     results = once(

time: 78.7 us -> 77.2 us (0.981)
  Pallas kernels: 27.4 us -> 26.1 us
    pallas_call x8, Pallas kernels: 16.1 us -> 14.9 us  [once(): pl.pallas_call(kernel, out_shape=outputs, in_specs=specs, out_specs=out_s...]
  transfers between devices with their start and end apart: 6 -> 6, of which waited for: 4 -> 3; matrix products, arithmetic and copies ran while one was open for 0% -> 0% of each run, Pallas kernels for 24% -> 24%
where the time goes in v3:
time: 77.2 us; the launch traced here: 76.8 us
  Pallas kernels  26.1 us (34%)
  starting transfers between devices  24 us (31%)
  blocking collectives  19.1 us (25%)
  waiting for transfers between devices  6.81 us (9%)
    all_to_all x1, blocking collectives, shards(): lax.all_to_all(entries, GROUP, split_axis=0, concat_axis=0, tiled=True)  19.1 us
    pallas_call x8, Pallas kernels, once(): pl.pallas_call(kernel, out_shape=outputs, in_specs=specs, out_specs=out_s...  14.9 us
    pallas_call x1, Pallas kernels, shards(): pl.pallas_call(inner_results, out_shape=[pltpu.HBM(queries.shape, BF16)]...  11.2 us
    ppermute x3, starting transfers between devices, shards(): lax.ppermute(total, 'zh', [(at, (at + distance) % size) for at in range(s...  9.67 us
    all_to_all x1, starting transfers between devices, shards(): lax.all_to_all(pairs, GROUP, split_axis=0, concat_axis=0, tiled=True)  6.67 us
    all_to_all x1, waiting for transfers between devices, shards(): lax.all_to_all(pairs, GROUP, split_axis=0, concat_axis=0, tiled=True)  4.57 us
    ppermute x1, starting transfers between devices, shards(): arrived = lax.ppermute(leaving, 'core', swap)  4.34 us
    ppermute x1, starting transfers between devices, shards(): other = lax.ppermute(sent, 'core', swap)  3.34 us
  transfers between devices with their start and end apart: 6, of which 3 were waited for; matrix products, arithmetic and copies ran while one was open for 0% of the time, Pallas kernels for 24%

profile of v3, /device:TPU:1, one launch (start us, length us, event | category | flops | bytes accessed | tf_op | source)
XLA Modules:
  0.0 76.8 jit_solution(17005288532167284672)
XLA Ops:
  0.6 0.0 copy-start
  0.6 3.6 %shard_map.84 = (bf16[16,264,128]{2,1,0:T(8,128)(2,1)S(1)}, bf16[128,2048]{1,0:T(8,128)(2,1)S(1)}, bf16[128,2048]{1,0:T(8,128)(2,1)S(1)}, bf16[128,2048]{1,0:T(8,128)(2,1)S(1)}, bf16[128,2048]{1,0:T(8,128)(2,1)S(1)}) custom-call(s32[1]{0:T(128)S(6)} %sub.3.half_ref, bf16[32,128]{1,0:T(8,128)(2,1)} %bitcast.3, bf16[128,4096]{1,0:T(8,128)(2,1)} %refs_0_.3, ...), custom_call_target="tpu_custom_call" | custom-call | tf_op jit(solution)/shard_map/pallas_call | solution.py:392
  4.3 3.3 %collective-permute-start = (bf16[16,264,128]{2,1,0:T(8,128)(2,1)S(1)}, bf16[16,264,128]{2,1,0:T(8,128)(2,1)S(1)}, u32[]{:S(2)}, u32[]{:S(2)}) collective-permute-start(bf16[16,264,128]{2,1,0:T(8,128)(2,1)S(1)} %get-tuple-element.41), channel_id=1, source_target_pairs={{0,1},{1,0},{2,3},{3,2},{4,5},{5,4},{6,7},{7,6},{8,9},{9,8},{10,11... | collective-permute-start | bytes 3244040 | tf_op jit(solution)/shard_map/ppermute | solution.py:433
  7.6 0.0 copy-done
  7.6 1.9 %shard_map.85.own_ref = f32[16,264,128]{2,1,0:T(8,128)S(1)} custom-call(s32[1]{0:T(128)} %bitcast.half_ref, bf16[32,128]{1,0:T(8,128)(2,1)S(1)} %bitcast.4, bf16[128,2048]{1,0:T(8,128)(2,1)S(1)} %get-tuple-element.37.refs_0_.refs_8_, bf16[128,2048]{1,0:T(8,128)(2,1)S(1)} %get-tuple-element.38.refs_1_.refs_9_, ...), custom_call_target="tpu_custom_call" | custom-call | tf_op jit(solution)/shard_map/pallas_call | solution.py:392
  9.5 0.5 collective-permute-done.other_ref
  10.0 1.2 %shard_map.86 = (bf16[32,136,128]{2,1,0:T(8,128)(2,1)}, bf16[16,136,128]{2,1,0:T(8,128)(2,1)S(1)}, bf16[16,136,128]{2,1,0:T(8,128)(2,1)S(1)}) custom-call(s32[1]{0:T(128)} %bitcast.half_ref, f32[16,264,128]{2,1,0:T(8,128)S(1)} %shard_map.85.own_ref, bf16[16,264,128]{2,1,0:T(8,128)(2,1)S(1)} %collective-permute-done.other_ref), custom_call_target="tpu_custom_call" | custom-call | tf_op jit(solution)/shard_map/pallas_call | solution.py:392
  11.2 6.7 %all-to-all-start = ((bf16[32,136,128]{2,1,0:T(8,128)(2,1)}), bf16[32,136,128]{2,1,0:T(8,128)(2,1)S(1)}, u32[]{:S(2)}, u32[]{:S(2)}) async-start(bf16[32,136,128]{2,1,0:T(8,128)(2,1)} %get-tuple-element.42), calls=%async_computation | async-start | bytes 2228224 | tf_op jit(solution)/shard_map/all_to_all | solution.py:441
  17.8 11.2 %shard_map.87 = (bf16[128,4096]{1,0:T(8,128)(2,1)}, bf16[128,4096]{1,0:T(8,128)(2,1)}, bf16[128,4096]{1,0:T(8,128)(2,1)}, bf16[128,4096]{1,0:T(8,128)(2,1)}) custom-call(bf16[32,128]{1,0:T(8,128)(2,1)S(1)} %bitcast.5, bf16[128,4096]{1,0:T(8,128)(2,1)} %refs_0_.3, bf16[128,4096]{1,0:T(8,128)(2,1)} %refs_1_.3, bf16[128,4096]{1,0:T(8,128)(2,1)} %refs_2_.3, ...), custom_call_target="tpu_custom_call" | custom-call | tf_op jit(solution)/shard_map/pallas_call | solution.py:444
  29.1 4.6 %all-to-all-done.pieces_ref = bf16[32,136,128]{2,1,0:T(8,128)(2,1)S(1)} async-done(((bf16[32,136,128]{2,1,0:T(8,128)(2,1)}), bf16[32,136,128]{2,1,0:T(8,128)(2,1)S(1)}, u32[]{:S(2)}, u32[]{:S(2)}) %all-to-all-start) | async-done | bytes 1114144 | tf_op jit(solution)/shard_map/all_to_all | solution.py:441
  33.6 0.3 shard_map.88
  34.0 6.1 %collective-permute-start.1 = (f32[72,128]{1,0:T(8,128)S(1)}, f32[72,128]{1,0:T(8,128)S(1)}, u32[]{:S(2)}, u32[]{:S(2)}) collective-permute-start(f32[72,128]{1,0:T(8,128)S(1)} %get-tuple-element.53), channel_id=1, source_target_pairs={{0,128},{64,192},{128,0},{192,64},{1,129},{65,193},{129,1},{193,65... | collective-permute-start | bytes 110600 | tf_op jit(solution)/shard_map/ppermute | solution.py:459
  40.1 1.2 %collective-permute-start.2 = (f32[72,128]{1,0:T(8,128)S(1)}, f32[72,128]{1,0:T(8,128)S(1)}, u32[]{:S(2)}, u32[]{:S(2)}) collective-permute-start(f32[72,128]{1,0:T(8,128)S(1)} %get-tuple-element.54), channel_id=1, source_target_pairs={{0,64},{64,128},{128,192},{192,0},{1,65},{65,129},{129,193},{193,1... | collective-permute-start | bytes 110600 | tf_op jit(solution)/shard_map/ppermute | solution.py:459
  41.3 2.4 %collective-permute-start.3 = (f32[72,128]{1,0:T(8,128)S(1)}, f32[72,128]{1,0:T(8,128)S(1)}, u32[]{:S(2)}, u32[]{:S(2)}) collective-permute-start(f32[72,128]{1,0:T(8,128)S(1)} %get-tuple-element.55), channel_id=1, source_target_pairs={{0,192},{64,0},{128,64},{192,128},{1,193},{65,1},{129,65},{193,129... | collective-permute-start | bytes 110600 | tf_op jit(solution)/shard_map/ppermute | solution.py:459
  43.7 0.0 collective-permute-done.1.two_ref
  43.7 1.8 %collective-permute-done.2.one_ref = f32[72,128]{1,0:T(8,128)S(1)} collective-permute-done((f32[72,128]{1,0:T(8,128)S(1)}, f32[72,128]{1,0:T(8,128)S(1)}, u32[]{:S(2)}, u32[]{:S(2)}) %collective-permute-start.2) | collective-permute-done | bytes 36896 | tf_op jit(solution)/shard_map/ppermute | solution.py:459
  45.4 0.0 collective-permute-done.3.three_ref
  45.4 0.4 shard_map.89
  45.8 19.1 %all_to_all.10.refs_10_.pair_ref = bf16[32,128,128]{2,1,0:T(8,128)(2,1)S(1)} all-to-all(bf16[32,128,128]{2,1,0:T(8,128)(2,1)S(1)} %shard_map.89), channel_id=1, replica_groups=mesh['zh'=4,'zl'=2,'y'=4,'x'=4,'core'=2] {'zl','y','x'}, dimensions={0} | all-to-all | bytes 2097152 | tf_op jit(solution)/shard_map/all_to_all | solution.py:465
  64.9 0.2 shard_map.91
  65.1 4.3 %collective-permute-start.4 = (bf16[16,256,128]{2,1,0:T(8,128)(2,1)S(1)}, bf16[16,256,128]{2,1,0:T(8,128)(2,1)S(1)}, u32[]{:S(2)}, u32[]{:S(2)}) collective-permute-start(bf16[16,256,128]{2,1,0:T(8,128)(2,1)S(1)} %shard_map.91), channel_id=1, source_target_pairs={{0,1},{1,0},{2,3},{3,2},{4,5},{5,4},{6,7},{7,6},{8,9},{9,8},{10,11... | collective-permute-start | bytes 3145736 | tf_op jit(solution)/shard_map/ppermute | solution.py:469
  69.4 5.0 %shard_map.90 = (bf16[128,4096]{1,0:T(8,128)(2,1)}, bf16[128,4096]{1,0:T(8,128)(2,1)}, bf16[128,4096]{1,0:T(8,128)(2,1)}, bf16[128,4096]{1,0:T(8,128)(2,1)}, bf1...) custom-call(s32[1]{0:T(128)} %bitcast.half_ref, ...), custom_call_target="tpu_custom_call" | custom-call | tf_op jit(solution)/shard_map/pallas_call | solution.py:392
  74.5 0.0 collective-permute-done.4.refs_8_
  74.5 2.3 %shard_map.92 = (bf16[128,4096]{1,0:T(8,128)(2,1)}, bf16[128,4096]{1,0:T(8,128)(2,1)}, bf16[128,4096]{1,0:T(8,128)(2,1)}, bf16[128,4096]{1,0:T(8,128)(2,1)}) custom-call(s32[1]{0:T(128)S(6)} %sub.3.half_ref, bf16[32,128]{1,0:T(8,128)(2,1)S(1)} %bitcast.7, ...), custom_call_target="tpu_custom_call", output_to_operand_aliasing={{0}: (11, {}), {1}: (12, {}), {2}: (13, {}), {3}: (14, {})} | custom-call | tf_op jit(solution)/shard_map/pallas_call | solution.py:392
Async XLA Ops:
  0.6 7.0 %copy-start = (bf16[128,32]{0,1:T(8,128)(2,1)S(1)}, bf16[128,32]{0,1:T(8,128)(2,1)}, u32[]{:S(2)}) copy-start(bf16[128,32]{0,1:T(8,128)(2,1)} %param.9) | copy-start | bytes 24580
  4.3 5.7 %collective-permute-start = (bf16[16,264,128]{2,1,0:T(8,128)(2,1)S(1)}, bf16[16,264,128]{2,1,0:T(8,128)(2,1)S(1)}, u32[]{:S(2)}, u32[]{:S(2)}) collective-permute-start(bf16[16,264,128]{2,1,0:T(8,128)(2,1)S(1)} %get-tuple-element.41), channel_id=1, source_target_pairs={{0,1},{1,0},{2,3},{3,2},{4,5},{5,4},{6,7},{7,6},{8,9},{9,8},{10,11... | collective-permute-start | bytes 3244040 | tf_op jit(solution)/shard_map/ppermute | solution.py:433
  11.2 22.5 %all-to-all-start = ((bf16[32,136,128]{2,1,0:T(8,128)(2,1)}), bf16[32,136,128]{2,1,0:T(8,128)(2,1)S(1)}, u32[]{:S(2)}, u32[]{:S(2)}) async-start(bf16[32,136,128]{2,1,0:T(8,128)(2,1)} %get-tuple-element.42), calls=%async_computation | async-start | bytes 2228224 | tf_op jit(solution)/shard_map/all_to_all | solution.py:441
  34.0 9.7 %collective-permute-start.1 = (f32[72,128]{1,0:T(8,128)S(1)}, f32[72,128]{1,0:T(8,128)S(1)}, u32[]{:S(2)}, u32[]{:S(2)}) collective-permute-start(f32[72,128]{1,0:T(8,128)S(1)} %get-tuple-element.53), channel_id=1, source_target_pairs={{0,128},{64,192},{128,0},{192,64},{1,129},{65,193},{129,1},{193,65... | collective-permute-start | bytes 110600 | tf_op jit(solution)/shard_map/ppermute | solution.py:459
  40.1 5.3 %collective-permute-start.2 = (f32[72,128]{1,0:T(8,128)S(1)}, f32[72,128]{1,0:T(8,128)S(1)}, u32[]{:S(2)}, u32[]{:S(2)}) collective-permute-start(f32[72,128]{1,0:T(8,128)S(1)} %get-tuple-element.54), channel_id=1, source_target_pairs={{0,64},{64,128},{128,192},{192,0},{1,65},{65,129},{129,193},{193,1... | collective-permute-start | bytes 110600 | tf_op jit(solution)/shard_map/ppermute | solution.py:459
  41.3 4.1 %collective-permute-start.3 = (f32[72,128]{1,0:T(8,128)S(1)}, f32[72,128]{1,0:T(8,128)S(1)}, u32[]{:S(2)}, u32[]{:S(2)}) collective-permute-start(f32[72,128]{1,0:T(8,128)S(1)} %get-tuple-element.55), channel_id=1, source_target_pairs={{0,192},{64,0},{128,64},{192,128},{1,193},{65,1},{129,65},{193,129... | collective-permute-start | bytes 110600 | tf_op jit(solution)/shard_map/ppermute | solution.py:459
  65.1 9.4 %collective-permute-start.4 = (bf16[16,256,128]{2,1,0:T(8,128)(2,1)S(1)}, bf16[16,256,128]{2,1,0:T(8,128)(2,1)S(1)}, u32[]{:S(2)}, u32[]{:S(2)}) collective-permute-start(bf16[16,256,128]{2,1,0:T(8,128)(2,1)S(1)} %shard_map.91), channel_id=1, source_target_pairs={{0,1},{1,0},{2,3},{3,2},{4,5},{5,4},{6,7},{7,6},{8,9},{9,8},{10,11... | collective-permute-start | bytes 3145736 | tf_op jit(solution)/shard_map/ppermute | solution.py:469

commit v4 on v3

--- a/solution.py
+++ b/solution.py
@@ -302,11 +302,10 @@
 def own_results(half_ref, decay_ref, *refs):
     held, refs = refs[:8], refs[8:]
     near, (pair_ref, their_ref), refs = refs[:HELD], refs[HELD : HELD + 2], refs[HELD + 2 :]
-    outs_hbm, refs = refs[:4], refs[4:]
+    outs, refs = refs[:4], refs[4:]
     away, refs = refs[:8], refs[8:]
     near, refs = near + refs[: 8 - HELD], refs[8 - HELD :]
-    outs, refs = refs[:4], refs[4:]
-    entry_ref, near_sems, away_sems, out_sems = refs
+    entry_ref, near_sems, away_sems = refs
     half = half_ref[0]
 
     def fetch(array, at):
@@ -323,7 +322,6 @@
             held[array].at[:, pl.ds(source, WIDTH)], away[array], away_sems.at[array]
         )
 
-    store = result_copies(half, outs_hbm, outs, out_sems)
     for array in range(HELD, 8):
         fetch(array, 0).start()
     fwd, bwd, _ = column_scales(half_decay(decay_ref, half))
@@ -337,29 +335,30 @@
         if spot == PER_STEP:
             for array in range(8):
                 fetch_away(array).start()
-        step, head = divmod(spot, PER_STEP)
         one = slice(spot, spot + 1)
         entry = entry_ref[spot]
         add_states(
             near[:4], near[4:], outs, spot, slice(spot * HEAD, (spot + 1) * HEAD),
             fwd[:, one], bwd[:, one], entry[0:HEAD], entry[HEAD:],
         )
-        if head == PER_STEP - 1:
-            for array in range(4):
-                store(array, step).start()
     for array in range(8):
         fetch_away(array).wait()
-    for step in range(STEPS):
-        for array in range(4):
-            store(array, step).wait()
 
 
 def other_results(half_ref, decay_ref, *refs):
-    away, entry_ref = refs[:8], refs[8]
-    outs_hbm, refs = refs[13:17], refs[17:]
-    outs, (out_sems,) = refs[:4], refs[4:]
+    away, entry_ref, ready = refs[:8], refs[8], refs[9:13]
+    outs_hbm, outs, (out_sems, ready_sems) = refs[13:17], refs[17:21], refs[21:]
     half = half_ref[0]
     store = result_copies(half, outs_hbm, outs, out_sems)
+
+    def store_ready(array):
+        target = pl.multiple_of((1 - half) * WIDTH, WIDTH)
+        return pltpu.make_async_copy(
+            ready[array], outs_hbm[array].at[:, pl.ds(target, WIDTH)], ready_sems.at[array]
+        )
+
+    for array in range(4):
+        store_ready(array).start()
     fwd, bwd, _ = column_scales(half_decay(decay_ref, half))
     for spot in range(HALF_HEADS):
         step, head = divmod(spot, PER_STEP)
@@ -372,6 +371,8 @@
         if head == PER_STEP - 1:
             for array in range(4):
                 store(array, step).start()
+    for array in range(4):
+        store_ready(array).wait()
     for step in range(STEPS):
         for array in range(4):
             store(array, step).wait()
@@ -467,25 +468,22 @@
         other_entries, (mine, own_part, pair_entries), pltpu.VMEM((HALF_HEADS, 2 * HEAD, HEAD), BF16)
     )
     arrived = lax.ppermute(leaving, "core", swap)
-    shapes = [pltpu.HBM(queries.shape, BF16)] * 4
     results = once(
         own_results, (mine, decay) + rows + inner + tuple(kept_rows[:HELD]) + (pair_entries, other_part),
-        shapes + list(buffers * 8),
-        buffers * (12 - HELD)
+        list(buffers * 12),
+        buffers * (8 - HELD)
         + (
             pltpu.VMEM((HALF_HEADS, 2 * HEAD, HEAD), BF16),
             pltpu.SemaphoreType.DMA((8, LOADS)),
             pltpu.SemaphoreType.DMA((8,)),
-            pltpu.SemaphoreType.DMA((4, STEPS)),
         ),
         [IN_SMEM, IN_VMEM] + [IN_HBM] * 8 + [IN_VMEM] * (2 + HELD),
-        [IN_HBM] * 4 + [IN_VMEM] * 8,
     )
     results = once(
-        other_results, (theirs, decay) + tuple(results[4:]) + (arrived,) + tuple(results[:4]), shapes,
-        buffers * 4 + (pltpu.SemaphoreType.DMA((4, STEPS)),),
-        [IN_SMEM] + [IN_VMEM] * 10 + [IN_HBM] * 4, [IN_HBM] * 4,
-        {11: 0, 12: 1, 13: 2, 14: 3},
+        other_results, (theirs, decay) + tuple(results[4:]) + (arrived,) + tuple(results[:4]),
+        [pltpu.HBM(queries.shape, BF16)] * 4,
+        buffers * 4 + (pltpu.SemaphoreType.DMA((4, STEPS)), pltpu.SemaphoreType.DMA((4,))),
+        out_specs=[IN_HBM] * 4,
     )
     return tuple(results)
 

time: 77.2 us -> 76.1 us (0.986)
  Pallas kernels: 26.1 us -> 24.9 us
    pallas_call x8, Pallas kernels: 14.9 us -> 13.7 us  [once(): pl.pallas_call(kernel, out_shape=outputs, in_specs=specs, out_specs=out_s...]
  transfers between devices with their start and end apart: 6 -> 6, of which waited for: 3 -> 3; matrix products, arithmetic and copies ran while one was open for 0% -> 0% of each run, Pallas kernels for 24% -> 22%
where the time goes in v4:
time: 76.1 us; the launch traced here: 75.6 us
  Pallas kernels  24.9 us (33%)
  starting transfers between devices  24 us (32%)
  blocking collectives  19.1 us (25%)
  waiting for transfers between devices  6.9 us (9%)
    all_to_all x1, blocking collectives, shards(): lax.all_to_all(entries, GROUP, split_axis=0, concat_axis=0, tiled=True)  19.1 us
    pallas_call x8, Pallas kernels, once(): pl.pallas_call(kernel, out_shape=outputs, in_specs=specs, out_specs=out_s...  13.7 us
    pallas_call x1, Pallas kernels, shards(): pl.pallas_call(inner_results, out_shape=[pltpu.HBM(queries.shape, BF16)]...  11.1 us
    ppermute x3, starting transfers between devices, shards(): lax.ppermute(total, 'zh', [(at, (at + distance) % size) for at in range(s...  9.67 us
    all_to_all x1, starting transfers between devices, shards(): lax.all_to_all(pairs, GROUP, split_axis=0, concat_axis=0, tiled=True)  6.67 us
    all_to_all x1, waiting for transfers between devices, shards(): lax.all_to_all(pairs, GROUP, split_axis=0, concat_axis=0, tiled=True)  4.67 us
    ppermute x1, starting transfers between devices, shards(): arrived = lax.ppermute(leaving, 'core', swap)  4.34 us
    ppermute x1, starting transfers between devices, shards(): other = lax.ppermute(sent, 'core', swap)  3.32 us
  transfers between devices with their start and end apart: 6, of which 3 were waited for; matrix products, arithmetic and copies ran while one was open for 0% of the time, Pallas kernels for 22%

profile of v4, /device:TPU:1, one launch (start us, length us, event | category | flops | bytes accessed | tf_op | source)
XLA Modules:
  0.0 75.6 jit_solution(10882585466880389822)
XLA Ops:
  0.6 0.0 copy-start
  0.6 3.6 %shard_map.84 = (bf16[16,264,128]{2,1,0:T(8,128)(2,1)S(1)}, bf16[128,2048]{1,0:T(8,128)(2,1)S(1)}, bf16[128,2048]{1,0:T(8,128)(2,1)S(1)}, bf16[128,2048]{1,0:T(8,128)(2,1)S(1)}, bf16[128,2048]{1,0:T(8,128)(2,1)S(1)}) custom-call(s32[1]{0:T(128)S(6)} %sub.3.half_ref, bf16[32,128]{1,0:T(8,128)(2,1)} %bitcast.3, bf16[128,4096]{1,0:T(8,128)(2,1)} %refs_0_.3, ...), custom_call_target="tpu_custom_call" | custom-call | tf_op jit(solution)/shard_map/pallas_call | solution.py:393
  4.3 3.3 %collective-permute-start = (bf16[16,264,128]{2,1,0:T(8,128)(2,1)S(1)}, bf16[16,264,128]{2,1,0:T(8,128)(2,1)S(1)}, u32[]{:S(2)}, u32[]{:S(2)}) collective-permute-start(bf16[16,264,128]{2,1,0:T(8,128)(2,1)S(1)} %get-tuple-element.41), channel_id=1, source_target_pairs={{0,1},{1,0},{2,3},{3,2},{4,5},{5,4},{6,7},{7,6},{8,9},{9,8},{10,11... | collective-permute-start | bytes 3244040 | tf_op jit(solution)/shard_map/ppermute | solution.py:434
  7.6 0.0 copy-done
  7.6 1.9 %shard_map.85.own_ref = f32[16,264,128]{2,1,0:T(8,128)S(1)} custom-call(s32[1]{0:T(128)} %bitcast.half_ref, bf16[32,128]{1,0:T(8,128)(2,1)S(1)} %bitcast.4, bf16[128,2048]{1,0:T(8,128)(2,1)S(1)} %get-tuple-element.37.refs_0_.refs_8_, bf16[128,2048]{1,0:T(8,128)(2,1)S(1)} %get-tuple-element.38.refs_1_.refs_9_, ...), custom_call_target="tpu_custom_call" | custom-call | tf_op jit(solution)/shard_map/pallas_call | solution.py:393
  9.5 0.5 collective-permute-done.other_ref
  9.9 1.2 %shard_map.86 = (bf16[32,136,128]{2,1,0:T(8,128)(2,1)}, bf16[16,136,128]{2,1,0:T(8,128)(2,1)S(1)}, bf16[16,136,128]{2,1,0:T(8,128)(2,1)S(1)}) custom-call(s32[1]{0:T(128)} %bitcast.half_ref, f32[16,264,128]{2,1,0:T(8,128)S(1)} %shard_map.85.own_ref, bf16[16,264,128]{2,1,0:T(8,128)(2,1)S(1)} %collective-permute-done.other_ref), custom_call_target="tpu_custom_call" | custom-call | tf_op jit(solution)/shard_map/pallas_call | solution.py:393
  11.1 6.7 %all-to-all-start = ((bf16[32,136,128]{2,1,0:T(8,128)(2,1)}), bf16[32,136,128]{2,1,0:T(8,128)(2,1)S(1)}, u32[]{:S(2)}, u32[]{:S(2)}) async-start(bf16[32,136,128]{2,1,0:T(8,128)(2,1)} %get-tuple-element.42), calls=%async_computation | async-start | bytes 2228224 | tf_op jit(solution)/shard_map/all_to_all | solution.py:442
  17.8 11.1 %shard_map.87 = (bf16[128,4096]{1,0:T(8,128)(2,1)}, bf16[128,4096]{1,0:T(8,128)(2,1)}, bf16[128,4096]{1,0:T(8,128)(2,1)}, bf16[128,4096]{1,0:T(8,128)(2,1)}) custom-call(bf16[32,128]{1,0:T(8,128)(2,1)S(1)} %bitcast.5, bf16[128,4096]{1,0:T(8,128)(2,1)} %refs_0_.3, bf16[128,4096]{1,0:T(8,128)(2,1)} %refs_1_.3, bf16[128,4096]{1,0:T(8,128)(2,1)} %refs_2_.3, ...), custom_call_target="tpu_custom_call" | custom-call | tf_op jit(solution)/shard_map/pallas_call | solution.py:445
  29.0 4.7 %all-to-all-done.pieces_ref = bf16[32,136,128]{2,1,0:T(8,128)(2,1)S(1)} async-done(((bf16[32,136,128]{2,1,0:T(8,128)(2,1)}), bf16[32,136,128]{2,1,0:T(8,128)(2,1)S(1)}, u32[]{:S(2)}, u32[]{:S(2)}) %all-to-all-start) | async-done | bytes 1114144 | tf_op jit(solution)/shard_map/all_to_all | solution.py:442
  33.6 0.3 shard_map.88
  34.0 6.1 %collective-permute-start.1 = (f32[72,128]{1,0:T(8,128)S(1)}, f32[72,128]{1,0:T(8,128)S(1)}, u32[]{:S(2)}, u32[]{:S(2)}) collective-permute-start(f32[72,128]{1,0:T(8,128)S(1)} %get-tuple-element.53), channel_id=1, source_target_pairs={{0,128},{64,192},{128,0},{192,64},{1,129},{65,193},{129,1},{193,65... | collective-permute-start | bytes 110600 | tf_op jit(solution)/shard_map/ppermute | solution.py:460
  40.1 1.2 %collective-permute-start.2 = (f32[72,128]{1,0:T(8,128)S(1)}, f32[72,128]{1,0:T(8,128)S(1)}, u32[]{:S(2)}, u32[]{:S(2)}) collective-permute-start(f32[72,128]{1,0:T(8,128)S(1)} %get-tuple-element.54), channel_id=1, source_target_pairs={{0,64},{64,128},{128,192},{192,0},{1,65},{65,129},{129,193},{193,1... | collective-permute-start | bytes 110600 | tf_op jit(solution)/shard_map/ppermute | solution.py:460
  41.3 2.4 %collective-permute-start.3 = (f32[72,128]{1,0:T(8,128)S(1)}, f32[72,128]{1,0:T(8,128)S(1)}, u32[]{:S(2)}, u32[]{:S(2)}) collective-permute-start(f32[72,128]{1,0:T(8,128)S(1)} %get-tuple-element.55), channel_id=1, source_target_pairs={{0,192},{64,0},{128,64},{192,128},{1,193},{65,1},{129,65},{193,129... | collective-permute-start | bytes 110600 | tf_op jit(solution)/shard_map/ppermute | solution.py:460
  43.6 0.0 collective-permute-done.1.two_ref
  43.6 1.8 %collective-permute-done.2.one_ref = f32[72,128]{1,0:T(8,128)S(1)} collective-permute-done((f32[72,128]{1,0:T(8,128)S(1)}, f32[72,128]{1,0:T(8,128)S(1)}, u32[]{:S(2)}, u32[]{:S(2)}) %collective-permute-start.2) | collective-permute-done | bytes 36896 | tf_op jit(solution)/shard_map/ppermute | solution.py:460
  45.4 0.0 collective-permute-done.3.three_ref
  45.4 0.4 shard_map.89
  45.8 19.1 %all_to_all.10.refs_10_.pair_ref = bf16[32,128,128]{2,1,0:T(8,128)(2,1)S(1)} all-to-all(bf16[32,128,128]{2,1,0:T(8,128)(2,1)S(1)} %shard_map.89), channel_id=1, replica_groups=mesh['zh'=4,'zl'=2,'y'=4,'x'=4,'core'=2] {'zl','y','x'}, dimensions={0} | all-to-all | bytes 2097152 | tf_op jit(solution)/shard_map/all_to_all | solution.py:466
  64.9 0.2 shard_map.91
  65.1 4.3 %collective-permute-start.4 = (bf16[16,256,128]{2,1,0:T(8,128)(2,1)S(1)}, bf16[16,256,128]{2,1,0:T(8,128)(2,1)S(1)}, u32[]{:S(2)}, u32[]{:S(2)}) collective-permute-start(bf16[16,256,128]{2,1,0:T(8,128)(2,1)S(1)} %shard_map.91), channel_id=1, source_target_pairs={{0,1},{1,0},{2,3},{3,2},{4,5},{5,4},{6,7},{7,6},{8,9},{9,8},{10,11... | collective-permute-start | bytes 3145736 | tf_op jit(solution)/shard_map/ppermute | solution.py:470
  69.4 3.9 %shard_map.90 = (bf16[128,2048]{1,0:T(8,128)(2,1)S(1)}, bf16[128,2048]{1,0:T(8,128)(2,1)S(1)}, bf16[128,2048]{1,0:T(8,128)(2,1)S(1)}, bf16[128,2048]{1,0:T(8,128...) custom-call(s32[1]{0:T(128)} %bitcast.half_ref, ...), custom_call_target="tpu_custom_call" | custom-call | tf_op jit(solution)/shard_map/pallas_call | solution.py:393
  73.3 0.0 collective-permute-done.4.refs_8_
  73.3 2.3 %shard_map.92 = (bf16[128,4096]{1,0:T(8,128)(2,1)}, bf16[128,4096]{1,0:T(8,128)(2,1)}, bf16[128,4096]{1,0:T(8,128)(2,1)}, bf16[128,4096]{1,0:T(8,128)(2,1)}) custom-call(s32[1]{0:T(128)S(6)} %sub.3.half_ref, bf16[32,128]{1,0:T(8,128)(2,1)S(1)} %bitcast.7, bf16[128,2048]{1,0:T(8,128)(2,1)S(1)} %get-tuple-element.57.refs_0_, ...), custom_call_target="tpu_custom_call" | custom-call | tf_op jit(solution)/shard_map/pallas_call | solution.py:393
Async XLA Ops:
  0.6 7.0 %copy-start = (bf16[128,32]{0,1:T(8,128)(2,1)S(1)}, bf16[128,32]{0,1:T(8,128)(2,1)}, u32[]{:S(2)}) copy-start(bf16[128,32]{0,1:T(8,128)(2,1)} %param.9) | copy-start | bytes 24580
  4.3 5.7 %collective-permute-start = (bf16[16,264,128]{2,1,0:T(8,128)(2,1)S(1)}, bf16[16,264,128]{2,1,0:T(8,128)(2,1)S(1)}, u32[]{:S(2)}, u32[]{:S(2)}) collective-permute-start(bf16[16,264,128]{2,1,0:T(8,128)(2,1)S(1)} %get-tuple-element.41), channel_id=1, source_target_pairs={{0,1},{1,0},{2,3},{3,2},{4,5},{5,4},{6,7},{7,6},{8,9},{9,8},{10,11... | collective-permute-start | bytes 3244040 | tf_op jit(solution)/shard_map/ppermute | solution.py:434
  11.1 22.5 %all-to-all-start = ((bf16[32,136,128]{2,1,0:T(8,128)(2,1)}), bf16[32,136,128]{2,1,0:T(8,128)(2,1)S(1)}, u32[]{:S(2)}, u32[]{:S(2)}) async-start(bf16[32,136,128]{2,1,0:T(8,128)(2,1)} %get-tuple-element.42), calls=%async_computation | async-start | bytes 2228224 | tf_op jit(solution)/shard_map/all_to_all | solution.py:442
  34.0 9.7 %collective-permute-start.1 = (f32[72,128]{1,0:T(8,128)S(1)}, f32[72,128]{1,0:T(8,128)S(1)}, u32[]{:S(2)}, u32[]{:S(2)}) collective-permute-start(f32[72,128]{1,0:T(8,128)S(1)} %get-tuple-element.53), channel_id=1, source_target_pairs={{0,128},{64,192},{128,0},{192,64},{1,129},{65,193},{129,1},{193,65... | collective-permute-start | bytes 110600 | tf_op jit(solution)/shard_map/ppermute | solution.py:460
  40.1 5.3 %collective-permute-start.2 = (f32[72,128]{1,0:T(8,128)S(1)}, f32[72,128]{1,0:T(8,128)S(1)}, u32[]{:S(2)}, u32[]{:S(2)}) collective-permute-start(f32[72,128]{1,0:T(8,128)S(1)} %get-tuple-element.54), channel_id=1, source_target_pairs={{0,64},{64,128},{128,192},{192,0},{1,65},{65,129},{129,193},{193,1... | collective-permute-start | bytes 110600 | tf_op jit(solution)/shard_map/ppermute | solution.py:460
  41.3 4.1 %collective-permute-start.3 = (f32[72,128]{1,0:T(8,128)S(1)}, f32[72,128]{1,0:T(8,128)S(1)}, u32[]{:S(2)}, u32[]{:S(2)}) collective-permute-start(f32[72,128]{1,0:T(8,128)S(1)} %get-tuple-element.55), channel_id=1, source_target_pairs={{0,192},{64,0},{128,64},{192,128},{1,193},{65,1},{129,65},{193,129... | collective-permute-start | bytes 110600 | tf_op jit(solution)/shard_map/ppermute | solution.py:460
  65.1 8.2 %collective-permute-start.4 = (bf16[16,256,128]{2,1,0:T(8,128)(2,1)S(1)}, bf16[16,256,128]{2,1,0:T(8,128)(2,1)S(1)}, u32[]{:S(2)}, u32[]{:S(2)}) collective-permute-start(bf16[16,256,128]{2,1,0:T(8,128)(2,1)S(1)} %shard_map.91), channel_id=1, source_target_pairs={{0,1},{1,0},{2,3},{3,2},{4,5},{5,4},{6,7},{7,6},{8,9},{9,8},{10,11... | collective-permute-start | bytes 3145736 | tf_op jit(solution)/shard_map/ppermute | solution.py:470

commit v5 on v4

--- a/solution.py
+++ b/solution.py
@@ -244,8 +244,18 @@
             out_ref[head, pl.ds(same_to, PART), :] = pair_ref[2 * head + part, pl.ds(same_from, PART), :]
 
 
-def other_entries(half_ref, mine_ref, pair_ref, out_ref):
+def other_entries(half_ref, mine_ref, pair_ref, *refs):
+    count = 8 - HELD
+    held, out_ref, early, sems = refs[:count], refs[count], refs[count + 1 : -1], refs[-1]
+    cols = pl.ds(pl.multiple_of(half_ref[0] * WIDTH, WIDTH), LOAD)
+    copies = [
+        pltpu.make_async_copy(held[at].at[:, cols], early[at], sems.at[at]) for at in range(count)
+    ]
+    for copy in copies:
+        copy.start()
     write_entries(half_ref[0], mine_ref, pair_ref, out_ref)
+    for copy in copies:
+        copy.wait()
 
 
 def inner_results(
@@ -301,19 +311,18 @@
 
 def own_results(half_ref, decay_ref, *refs):
     held, refs = refs[:8], refs[8:]
-    near, (pair_ref, their_ref), refs = refs[:HELD], refs[HELD : HELD + 2], refs[HELD + 2 :]
+    kept, early, refs = refs[:HELD], refs[HELD:8], refs[8:]
+    (pair_ref, their_ref), refs = refs[:2], refs[2:]
     outs, refs = refs[:4], refs[4:]
     away, refs = refs[:8], refs[8:]
-    near, refs = near + refs[: 8 - HELD], refs[8 - HELD :]
+    late, refs = refs[: 8 - HELD], refs[8 - HELD :]
     entry_ref, near_sems, away_sems = refs
     half = half_ref[0]
 
-    def fetch(array, at):
-        source = pl.multiple_of(half * WIDTH + at * LOAD, LOAD)
+    def fetch(array):
+        source = pl.multiple_of(half * WIDTH + LOAD, LOAD)
         return pltpu.make_async_copy(
-            held[array].at[:, pl.ds(source, LOAD)],
-            near[array].at[:, at * LOAD : (at + 1) * LOAD],
-            near_sems.at[array, at],
+            held[array].at[:, pl.ds(source, LOAD)], late[array - HELD], near_sems.at[array]
         )
 
     def fetch_away(array):
@@ -323,22 +332,23 @@
         )
 
     for array in range(HELD, 8):
-        fetch(array, 0).start()
+        fetch(array).start()
     fwd, bwd, _ = column_scales(half_decay(decay_ref, half))
     write_entries(1 - half, their_ref, pair_ref, entry_ref)
-    for array in range(HELD, 8):
-        fetch(array, 1).start()
+    for array in range(8):
+        fetch_away(array).start()
     for spot in range(HALF_HEADS):
-        if spot % (HALF_HEADS // LOADS) == 0:
+        if spot == LOAD // HEAD:
             for array in range(HELD, 8):
-                fetch(array, spot // (HALF_HEADS // LOADS)).wait()
-        if spot == PER_STEP:
-            for array in range(8):
-                fetch_away(array).start()
+                fetch(array).wait()
+        rows = [ref.at[:, : LOAD] for ref in kept] + list(early)
+        if spot >= LOAD // HEAD:
+            rows = [ref.at[:, LOAD:] for ref in kept] + list(late)
+        from_at = spot * HEAD % LOAD
         one = slice(spot, spot + 1)
         entry = entry_ref[spot]
         add_states(
-            near[:4], near[4:], outs, spot, slice(spot * HEAD, (spot + 1) * HEAD),
+            rows[:4], rows[4:], outs, from_at // HEAD, slice(spot * HEAD, (spot + 1) * HEAD),
             fwd[:, one], bwd[:, one], entry[0:HEAD], entry[HEAD:],
         )
     for array in range(8):
@@ -464,20 +474,25 @@
         group_entries, (place, pieces, *moved), pltpu.VMEM((2 * HALF_HEADS, 2 * PART, HEAD), BF16)
     )
     pair_entries = lax.all_to_all(entries, GROUP, split_axis=0, concat_axis=0, tiled=True)
-    leaving = once(
-        other_entries, (mine, own_part, pair_entries), pltpu.VMEM((HALF_HEADS, 2 * HEAD, HEAD), BF16)
+    short = (pltpu.VMEM((BLOCK, LOAD), BF16),) * (8 - HELD)
+    leaving, *early = once(
+        other_entries, (mine, own_part, pair_entries) + (rows + inner)[HELD:],
+        [pltpu.VMEM((HALF_HEADS, 2 * HEAD, HEAD), BF16)] + list(short),
+        (pltpu.SemaphoreType.DMA((8 - HELD,)),),
+        [IN_SMEM] + [IN_VMEM] * 2 + [IN_HBM] * (8 - HELD),
     )
     arrived = lax.ppermute(leaving, "core", swap)
     results = once(
-        own_results, (mine, decay) + rows + inner + tuple(kept_rows[:HELD]) + (pair_entries, other_part),
+        own_results,
+        (mine, decay) + rows + inner + tuple(kept_rows[:HELD]) + tuple(early) + (pair_entries, other_part),
         list(buffers * 12),
-        buffers * (8 - HELD)
+        short
         + (
             pltpu.VMEM((HALF_HEADS, 2 * HEAD, HEAD), BF16),
-            pltpu.SemaphoreType.DMA((8, LOADS)),
+            pltpu.SemaphoreType.DMA((8,)),
             pltpu.SemaphoreType.DMA((8,)),
         ),
-        [IN_SMEM, IN_VMEM] + [IN_HBM] * 8 + [IN_VMEM] * (2 + HELD),
+        [IN_SMEM, IN_VMEM] + [IN_HBM] * 8 + [IN_VMEM] * 10,
     )
     results = once(
         other_results, (theirs, decay) + tuple(results[4:]) + (arrived,) + tuple(results[:4]),

time: 76.1 us -> 77.4 us (1.017)
  Pallas kernels: 24.9 us -> 26.2 us
    pallas_call x8, Pallas kernels: 13.7 us -> 15.1 us  [once(): pl.pallas_call(kernel, out_shape=outputs, in_specs=specs, out_specs=out_s...]
where the time goes in v5:
time: 77.4 us; the launch traced here: 76.9 us
  Pallas kernels  26.2 us (34%)
  starting transfers between devices  24 us (31%)
  blocking collectives  19.1 us (25%)
  waiting for transfers between devices  6.9 us (9%)
    all_to_all x1, blocking collectives, shards(): lax.all_to_all(entries, GROUP, split_axis=0, concat_axis=0, tiled=True)  19.1 us
    pallas_call x8, Pallas kernels, once(): pl.pallas_call(kernel, out_shape=outputs, in_specs=specs, out_specs=out_s...  15.1 us
    pallas_call x1, Pallas kernels, shards(): pl.pallas_call(inner_results, out_shape=[pltpu.HBM(queries.shape, BF16)]...  11.1 us
    ppermute x3, starting transfers between devices, shards(): lax.ppermute(total, 'zh', [(at, (at + distance) % size) for at in range(s...  9.67 us
    all_to_all x1, starting transfers between devices, shards(): lax.all_to_all(pairs, GROUP, split_axis=0, concat_axis=0, tiled=True)  6.67 us
    all_to_all x1, waiting for transfers between devices, shards(): lax.all_to_all(pairs, GROUP, split_axis=0, concat_axis=0, tiled=True)  4.67 us
    ppermute x1, starting transfers between devices, shards(): arrived = lax.ppermute(leaving, 'core', swap)  4.34 us
    ppermute x1, starting transfers between devices, shards(): other = lax.ppermute(sent, 'core', swap)  3.32 us
  transfers between devices with their start and end apart: 6, of which 3 were waited for; matrix products, arithmetic and copies ran while one was open for 0% of the time, Pallas kernels for 22%

profile of v5, /device:TPU:1, one launch (start us, length us, event | category | flops | bytes accessed | tf_op | source)
XLA Modules:
  0.0 76.9 jit_solution(8834170328528668097)
XLA Ops:
  0.6 0.0 copy-start
  0.6 3.6 %shard_map.84 = (bf16[16,264,128]{2,1,0:T(8,128)(2,1)S(1)}, bf16[128,2048]{1,0:T(8,128)(2,1)S(1)}, bf16[128,2048]{1,0:T(8,128)(2,1)S(1)}, bf16[128,2048]{1,0:T(8,128)(2,1)S(1)}, bf16[128,2048]{1,0:T(8,128)(2,1)S(1)}) custom-call(s32[1]{0:T(128)S(6)} %sub.3.half_ref, bf16[32,128]{1,0:T(8,128)(2,1)} %bitcast.3, bf16[128,4096]{1,0:T(8,128)(2,1)} %refs_0_.5, ...), custom_call_target="tpu_custom_call" | custom-call | tf_op jit(solution)/shard_map/pallas_call | solution.py:403
  4.3 3.3 %collective-permute-start = (bf16[16,264,128]{2,1,0:T(8,128)(2,1)S(1)}, bf16[16,264,128]{2,1,0:T(8,128)(2,1)S(1)}, u32[]{:S(2)}, u32[]{:S(2)}) collective-permute-start(bf16[16,264,128]{2,1,0:T(8,128)(2,1)S(1)} %get-tuple-element.48), channel_id=1, source_target_pairs={{0,1},{1,0},{2,3},{3,2},{4,5},{5,4},{6,7},{7,6},{8,9},{9,8},{10,11... | collective-permute-start | bytes 3244040 | tf_op jit(solution)/shard_map/ppermute | solution.py:444
  7.6 0.0 copy-done
  7.6 1.9 %shard_map.85.own_ref = f32[16,264,128]{2,1,0:T(8,128)S(1)} custom-call(s32[1]{0:T(128)} %bitcast.half_ref, bf16[32,128]{1,0:T(8,128)(2,1)S(1)} %bitcast.4, bf16[128,2048]{1,0:T(8,128)(2,1)S(1)} %get-tuple-element.44.refs_0_.refs_8_, bf16[128,2048]{1,0:T(8,128)(2,1)S(1)} %get-tuple-element.45.refs_1_.refs_9_, ...), custom_call_target="tpu_custom_call" | custom-call | tf_op jit(solution)/shard_map/pallas_call | solution.py:403
  9.5 0.5 collective-permute-done.other_ref
  9.9 1.2 %shard_map.86 = (bf16[32,136,128]{2,1,0:T(8,128)(2,1)}, bf16[16,136,128]{2,1,0:T(8,128)(2,1)S(1)}, bf16[16,136,128]{2,1,0:T(8,128)(2,1)S(1)}) custom-call(s32[1]{0:T(128)} %bitcast.half_ref, f32[16,264,128]{2,1,0:T(8,128)S(1)} %shard_map.85.own_ref, bf16[16,264,128]{2,1,0:T(8,128)(2,1)S(1)} %collective-permute-done.other_ref), custom_call_target="tpu_custom_call" | custom-call | tf_op jit(solution)/shard_map/pallas_call | solution.py:403
  11.1 6.7 %all-to-all-start = ((bf16[32,136,128]{2,1,0:T(8,128)(2,1)}), bf16[32,136,128]{2,1,0:T(8,128)(2,1)S(1)}, u32[]{:S(2)}, u32[]{:S(2)}) async-start(bf16[32,136,128]{2,1,0:T(8,128)(2,1)} %get-tuple-element.49), calls=%async_computation | async-start | bytes 2228224 | tf_op jit(solution)/shard_map/all_to_all | solution.py:452
  17.8 11.1 %shard_map.87 = (bf16[128,4096]{1,0:T(8,128)(2,1)}, bf16[128,4096]{1,0:T(8,128)(2,1)}, bf16[128,4096]{1,0:T(8,128)(2,1)}, bf16[128,4096]{1,0:T(8,128)(2,1)}) custom-call(bf16[32,128]{1,0:T(8,128)(2,1)S(1)} %bitcast.5, bf16[128,4096]{1,0:T(8,128)(2,1)} %refs_0_.5, bf16[128,4096]{1,0:T(8,128)(2,1)} %refs_1_.5, bf16[128,4096]{1,0:T(8,128)(2,1)} %refs_2_.3, ...), custom_call_target="tpu_custom_call" | custom-call | tf_op jit(solution)/shard_map/pallas_call | solution.py:455
  29.0 4.7 %all-to-all-done.pieces_ref = bf16[32,136,128]{2,1,0:T(8,128)(2,1)S(1)} async-done(((bf16[32,136,128]{2,1,0:T(8,128)(2,1)}), bf16[32,136,128]{2,1,0:T(8,128)(2,1)S(1)}, u32[]{:S(2)}, u32[]{:S(2)}) %all-to-all-start) | async-done | bytes 1114144 | tf_op jit(solution)/shard_map/all_to_all | solution.py:452
  33.6 0.3 shard_map.88
  34.0 6.1 %collective-permute-start.1 = (f32[72,128]{1,0:T(8,128)S(1)}, f32[72,128]{1,0:T(8,128)S(1)}, u32[]{:S(2)}, u32[]{:S(2)}) collective-permute-start(f32[72,128]{1,0:T(8,128)S(1)} %get-tuple-element.61), channel_id=1, source_target_pairs={{0,128},{64,192},{128,0},{192,64},{1,129},{65,193},{129,1},{193,65... | collective-permute-start | bytes 110600 | tf_op jit(solution)/shard_map/ppermute | solution.py:470
  40.1 1.2 %collective-permute-start.2 = (f32[72,128]{1,0:T(8,128)S(1)}, f32[72,128]{1,0:T(8,128)S(1)}, u32[]{:S(2)}, u32[]{:S(2)}) collective-permute-start(f32[72,128]{1,0:T(8,128)S(1)} %get-tuple-element.62), channel_id=1, source_target_pairs={{0,64},{64,128},{128,192},{192,0},{1,65},{65,129},{129,193},{193,1... | collective-permute-start | bytes 110600 | tf_op jit(solution)/shard_map/ppermute | solution.py:470
  41.3 2.4 %collective-permute-start.3 = (f32[72,128]{1,0:T(8,128)S(1)}, f32[72,128]{1,0:T(8,128)S(1)}, u32[]{:S(2)}, u32[]{:S(2)}) collective-permute-start(f32[72,128]{1,0:T(8,128)S(1)} %get-tuple-element.63), channel_id=1, source_target_pairs={{0,192},{64,0},{128,64},{192,128},{1,193},{65,1},{129,65},{193,129... | collective-permute-start | bytes 110600 | tf_op jit(solution)/shard_map/ppermute | solution.py:470
  43.6 0.0 collective-permute-done.1.two_ref
  43.6 1.8 %collective-permute-done.2.one_ref = f32[72,128]{1,0:T(8,128)S(1)} collective-permute-done((f32[72,128]{1,0:T(8,128)S(1)}, f32[72,128]{1,0:T(8,128)S(1)}, u32[]{:S(2)}, u32[]{:S(2)}) %collective-permute-start.2) | collective-permute-done | bytes 36896 | tf_op jit(solution)/shard_map/ppermute | solution.py:470
  45.4 0.0 collective-permute-done.3.three_ref
  45.4 0.4 shard_map.89
  45.8 19.1 %all_to_all.10.pair_ref.refs_16_ = bf16[32,128,128]{2,1,0:T(8,128)(2,1)S(1)} all-to-all(bf16[32,128,128]{2,1,0:T(8,128)(2,1)S(1)} %shard_map.89), channel_id=1, replica_groups=mesh['zh'=4,'zl'=2,'y'=4,'x'=4,'core'=2] {'zl','y','x'}, dimensions={0} | all-to-all | bytes 2097152 | tf_op jit(solution)/shard_map/all_to_all | solution.py:476
  64.9 1.4 %shard_map.90 = (bf16[16,256,128]{2,1,0:T(8,128)(2,1)S(1)}, bf16[128,1024]{1,0:T(8,128)(2,1)S(1)}, bf16[128,1024]{1,0:T(8,128)(2,1)S(1)}, bf16[128,1024]{1,0:T(8...) custom-call(s32[1]{0:T(128)} %bitcast.half_ref, ...), custom_call_target="tpu_custom_call" | custom-call | tf_op jit(solution)/shard_map/pallas_call | solution.py:403
  66.3 4.3 %collective-permute-start.4 = (bf16[16,256,128]{2,1,0:T(8,128)(2,1)S(1)}, bf16[16,256,128]{2,1,0:T(8,128)(2,1)S(1)}, u32[]{:S(2)}, u32[]{:S(2)}) collective-permute-start(bf16[16,256,128]{2,1,0:T(8,128)(2,1)S(1)} %get-tuple-element.79), channel_id=1, source_target_pairs={{0,1},{1,0},{2,3},{3,2},{4,5},{5,4},{6,7},{7,6},{8,9},{9,8},{10,11... | collective-permute-start | bytes 3145736 | tf_op jit(solution)/shard_map/ppermute | solution.py:484
  70.6 4.0 %shard_map.91 = (bf16[128,2048]{1,0:T(8,128)(2,1)S(1)}, bf16[128,2048]{1,0:T(8,128)(2,1)S(1)}, bf16[128,2048]{1,0:T(8,128)(2,1)S(1)}, bf16[128,2048]{1,0:T(8,128...) custom-call(s32[1]{0:T(128)} %bitcast.half_ref, ...), custom_call_target="tpu_custom_call" | custom-call | tf_op jit(solution)/shard_map/pallas_call | solution.py:403
  74.6 0.0 collective-permute-done.4.refs_8_
  74.6 2.3 %shard_map.92 = (bf16[128,4096]{1,0:T(8,128)(2,1)}, bf16[128,4096]{1,0:T(8,128)(2,1)}, bf16[128,4096]{1,0:T(8,128)(2,1)}, bf16[128,4096]{1,0:T(8,128)(2,1)}) custom-call(s32[1]{0:T(128)S(6)} %sub.3.half_ref, bf16[32,128]{1,0:T(8,128)(2,1)S(1)} %bitcast.7, bf16[128,2048]{1,0:T(8,128)(2,1)S(1)} %get-tuple-element.71.refs_0_, ...), custom_call_target="tpu_custom_call" | custom-call | tf_op jit(solution)/shard_map/pallas_call | solution.py:403
Async XLA Ops:
  0.6 7.0 %copy-start = (bf16[128,32]{0,1:T(8,128)(2,1)S(1)}, bf16[128,32]{0,1:T(8,128)(2,1)}, u32[]{:S(2)}) copy-start(bf16[128,32]{0,1:T(8,128)(2,1)} %param.9) | copy-start | bytes 24580
  4.3 5.7 %collective-permute-start = (bf16[16,264,128]{2,1,0:T(8,128)(2,1)S(1)}, bf16[16,264,128]{2,1,0:T(8,128)(2,1)S(1)}, u32[]{:S(2)}, u32[]{:S(2)}) collective-permute-start(bf16[16,264,128]{2,1,0:T(8,128)(2,1)S(1)} %get-tuple-element.48), channel_id=1, source_target_pairs={{0,1},{1,0},{2,3},{3,2},{4,5},{5,4},{6,7},{7,6},{8,9},{9,8},{10,11... | collective-permute-start | bytes 3244040 | tf_op jit(solution)/shard_map/ppermute | solution.py:444
  11.1 22.5 %all-to-all-start = ((bf16[32,136,128]{2,1,0:T(8,128)(2,1)}), bf16[32,136,128]{2,1,0:T(8,128)(2,1)S(1)}, u32[]{:S(2)}, u32[]{:S(2)}) async-start(bf16[32,136,128]{2,1,0:T(8,128)(2,1)} %get-tuple-element.49), calls=%async_computation | async-start | bytes 2228224 | tf_op jit(solution)/shard_map/all_to_all | solution.py:452
  34.0 9.7 %collective-permute-start.1 = (f32[72,128]{1,0:T(8,128)S(1)}, f32[72,128]{1,0:T(8,128)S(1)}, u32[]{:S(2)}, u32[]{:S(2)}) collective-permute-start(f32[72,128]{1,0:T(8,128)S(1)} %get-tuple-element.61), channel_id=1, source_target_pairs={{0,128},{64,192},{128,0},{192,64},{1,129},{65,193},{129,1},{193,65... | collective-permute-start | bytes 110600 | tf_op jit(solution)/shard_map/ppermute | solution.py:470
  40.1 5.3 %collective-permute-start.2 = (f32[72,128]{1,0:T(8,128)S(1)}, f32[72,128]{1,0:T(8,128)S(1)}, u32[]{:S(2)}, u32[]{:S(2)}) collective-permute-start(f32[72,128]{1,0:T(8,128)S(1)} %get-tuple-element.62), channel_id=1, source_target_pairs={{0,64},{64,128},{128,192},{192,0},{1,65},{65,129},{129,193},{193,1... | collective-permute-start | bytes 110600 | tf_op jit(solution)/shard_map/ppermute | solution.py:470
  41.3 4.1 %collective-permute-start.3 = (f32[72,128]{1,0:T(8,128)S(1)}, f32[72,128]{1,0:T(8,128)S(1)}, u32[]{:S(2)}, u32[]{:S(2)}) collective-permute-start(f32[72,128]{1,0:T(8,128)S(1)} %get-tuple-element.63), channel_id=1, source_target_pairs={{0,192},{64,0},{128,64},{192,128},{1,193},{65,1},{129,65},{193,129... | collective-permute-start | bytes 110600 | tf_op jit(solution)/shard_map/ppermute | solution.py:470
  66.3 8.3 %collective-permute-start.4 = (bf16[16,256,128]{2,1,0:T(8,128)(2,1)S(1)}, bf16[16,256,128]{2,1,0:T(8,128)(2,1)S(1)}, u32[]{:S(2)}, u32[]{:S(2)}) collective-permute-start(bf16[16,256,128]{2,1,0:T(8,128)(2,1)S(1)} %get-tuple-element.79), channel_id=1, source_target_pairs={{0,1},{1,0},{2,3},{3,2},{4,5},{5,4},{6,7},{7,6},{8,9},{9,8},{10,11... | collective-permute-start | bytes 3145736 | tf_op jit(solution)/shard_map/ppermute | solution.py:484

commit v6 on v4

--- a/solution.py
+++ b/solution.py
@@ -197,9 +197,9 @@
     state, trail, total = lax.fori_loop(
         0, count, hop, (zero, zero, jnp.zeros((1, HEAD), F32)), unroll=8
     )
-    tail = jnp.broadcast_to(total, (TAIL, HEAD))
+    tail = pack_decay(total)
     for distance, ref in zip(DISTANCES, outs):
-        ref[0:PART, :] = jnp.where(place + distance <= len(outs), state, trail)
+        ref[0:PART, :] = jnp.where(place + distance <= len(outs), state, trail).astype(BF16)
         ref[PART:, :] = tail
 
 
@@ -209,10 +209,10 @@
     state = jnp.zeros((PART, HEAD), F32)
     trail = jnp.zeros((PART, HEAD), F32)
     for distance, ref in ((3, three_ref), (2, two_ref), (1, one_ref)):
-        longer = jnp.exp(ref[PART : PART + 1, :]) * state + ref[0:PART, :]
+        longer = jnp.exp(unpack_decay(ref[PART:, :])) * state + ref[0:PART, :].astype(F32)
         state = jnp.where(place >= distance, longer, state)
     for distance, ref in ((1, one_ref), (2, two_ref), (3, three_ref)):
-        longer = jnp.exp(ref[PART : PART + 1, :]) * trail + ref[0:PART, :]
+        longer = jnp.exp(unpack_decay(ref[PART:, :])) * trail + ref[0:PART, :].astype(F32)
         trail = jnp.where(place < distance, longer, trail)
 
     def hop(at, carry):
@@ -455,7 +455,7 @@
     pieces, inner = lax.optimization_barrier((pieces, inner))
     inner = tuple(in_hbm(item) for item in inner)
     size = lax.axis_size("zh")
-    totals = once(group_total, (place, pieces), [pltpu.VMEM((PART + TAIL, HEAD), F32)] * (size - 1))
+    totals = once(group_total, (place, pieces), [pltpu.VMEM((PART + TAIL, HEAD), BF16)] * (size - 1))
     moved = [
         lax.ppermute(total, "zh", [(at, (at + distance) % size) for at in range(size)])
         for distance, total in zip(DISTANCES, totals)

time: 76.1 us -> 75.9 us (level)
  transfers between devices with their start and end apart: 6 -> 6, of which waited for: 3 -> 4; matrix products, arithmetic and copies ran while one was open for 0% -> 0% of each run, Pallas kernels for 22% -> 22%
where the time goes in v6:
time: 75.9 us; the launch traced here: 75.4 us
  Pallas kernels  24.9 us (33%)
  starting transfers between devices  24 us (32%)
  blocking collectives  19.3 us (25%)
  waiting for transfers between devices  6.46 us (9%)
    all_to_all x1, blocking collectives, shards(): lax.all_to_all(entries, GROUP, split_axis=0, concat_axis=0, tiled=True)  19.3 us
    pallas_call x8, Pallas kernels, once(): pl.pallas_call(kernel, out_shape=outputs, in_specs=specs, out_specs=out_s...  13.7 us
    pallas_call x1, Pallas kernels, shards(): pl.pallas_call(inner_results, out_shape=[pltpu.HBM(queries.shape, BF16)]...  11.1 us
    ppermute x3, starting transfers between devices, shards(): lax.ppermute(total, 'zh', [(at, (at + distance) % size) for at in range(s...  9.67 us
    all_to_all x1, starting transfers between devices, shards(): lax.all_to_all(pairs, GROUP, split_axis=0, concat_axis=0, tiled=True)  6.67 us
    all_to_all x1, waiting for transfers between devices, shards(): lax.all_to_all(pairs, GROUP, split_axis=0, concat_axis=0, tiled=True)  4.67 us
    ppermute x1, starting transfers between devices, shards(): arrived = lax.ppermute(leaving, 'core', swap)  4.34 us
    ppermute x1, starting transfers between devices, shards(): other = lax.ppermute(sent, 'core', swap)  3.32 us
  transfers between devices with their start and end apart: 6, of which 4 were waited for; matrix products, arithmetic and copies ran while one was open for 0% of the time, Pallas kernels for 22%

profile of v6, /device:TPU:1, one launch (start us, length us, event | category | flops | bytes accessed | tf_op | source)
XLA Modules:
  0.0 75.4 jit_solution(2054527754320897046)
XLA Ops:
  0.6 0.0 copy-start
  0.6 3.6 %shard_map.84 = (bf16[16,264,128]{2,1,0:T(8,128)(2,1)S(1)}, bf16[128,2048]{1,0:T(8,128)(2,1)S(1)}, bf16[128,2048]{1,0:T(8,128)(2,1)S(1)}, bf16[128,2048]{1,0:T(8,128)(2,1)S(1)}, bf16[128,2048]{1,0:T(8,128)(2,1)S(1)}) custom-call(s32[1]{0:T(128)S(6)} %sub.3.half_ref, bf16[32,128]{1,0:T(8,128)(2,1)} %bitcast.3, bf16[128,4096]{1,0:T(8,128)(2,1)} %refs_0_.3, ...), custom_call_target="tpu_custom_call" | custom-call | tf_op jit(solution)/shard_map/pallas_call | solution.py:393
  4.3 3.3 %collective-permute-start = (bf16[16,264,128]{2,1,0:T(8,128)(2,1)S(1)}, bf16[16,264,128]{2,1,0:T(8,128)(2,1)S(1)}, u32[]{:S(2)}, u32[]{:S(2)}) collective-permute-start(bf16[16,264,128]{2,1,0:T(8,128)(2,1)S(1)} %get-tuple-element.41), channel_id=1, source_target_pairs={{0,1},{1,0},{2,3},{3,2},{4,5},{5,4},{6,7},{7,6},{8,9},{9,8},{10,11... | collective-permute-start | bytes 3244040 | tf_op jit(solution)/shard_map/ppermute | solution.py:434
  7.6 0.0 copy-done
  7.6 1.9 %shard_map.85.own_ref = f32[16,264,128]{2,1,0:T(8,128)S(1)} custom-call(s32[1]{0:T(128)} %bitcast.half_ref, bf16[32,128]{1,0:T(8,128)(2,1)S(1)} %bitcast.4, bf16[128,2048]{1,0:T(8,128)(2,1)S(1)} %get-tuple-element.37.refs_0_.refs_8_, bf16[128,2048]{1,0:T(8,128)(2,1)S(1)} %get-tuple-element.38.refs_1_.refs_9_, ...), custom_call_target="tpu_custom_call" | custom-call | tf_op jit(solution)/shard_map/pallas_call | solution.py:393
  9.5 0.5 collective-permute-done.other_ref
  9.9 1.2 %shard_map.86 = (bf16[32,136,128]{2,1,0:T(8,128)(2,1)}, bf16[16,136,128]{2,1,0:T(8,128)(2,1)S(1)}, bf16[16,136,128]{2,1,0:T(8,128)(2,1)S(1)}) custom-call(s32[1]{0:T(128)} %bitcast.half_ref, f32[16,264,128]{2,1,0:T(8,128)S(1)} %shard_map.85.own_ref, bf16[16,264,128]{2,1,0:T(8,128)(2,1)S(1)} %collective-permute-done.other_ref), custom_call_target="tpu_custom_call" | custom-call | tf_op jit(solution)/shard_map/pallas_call | solution.py:393
  11.1 6.7 %all-to-all-start = ((bf16[32,136,128]{2,1,0:T(8,128)(2,1)}), bf16[32,136,128]{2,1,0:T(8,128)(2,1)S(1)}, u32[]{:S(2)}, u32[]{:S(2)}) async-start(bf16[32,136,128]{2,1,0:T(8,128)(2,1)} %get-tuple-element.42), calls=%async_computation | async-start | bytes 2228224 | tf_op jit(solution)/shard_map/all_to_all | solution.py:442
  17.8 11.1 %shard_map.87 = (bf16[128,4096]{1,0:T(8,128)(2,1)}, bf16[128,4096]{1,0:T(8,128)(2,1)}, bf16[128,4096]{1,0:T(8,128)(2,1)}, bf16[128,4096]{1,0:T(8,128)(2,1)}) custom-call(bf16[32,128]{1,0:T(8,128)(2,1)S(1)} %bitcast.5, bf16[128,4096]{1,0:T(8,128)(2,1)} %refs_0_.3, bf16[128,4096]{1,0:T(8,128)(2,1)} %refs_1_.3, bf16[128,4096]{1,0:T(8,128)(2,1)} %refs_2_.3, ...), custom_call_target="tpu_custom_call" | custom-call | tf_op jit(solution)/shard_map/pallas_call | solution.py:445
  29.0 4.7 %all-to-all-done.pieces_ref = bf16[32,136,128]{2,1,0:T(8,128)(2,1)S(1)} async-done(((bf16[32,136,128]{2,1,0:T(8,128)(2,1)}), bf16[32,136,128]{2,1,0:T(8,128)(2,1)S(1)}, u32[]{:S(2)}, u32[]{:S(2)}) %all-to-all-start) | async-done | bytes 1114144 | tf_op jit(solution)/shard_map/all_to_all | solution.py:442
  33.6 0.3 shard_map.88
  34.0 6.1 %collective-permute-start.1 = (bf16[72,128]{1,0:T(8,128)(2,1)S(1)}, bf16[72,128]{1,0:T(8,128)(2,1)S(1)}, u32[]{:S(2)}, u32[]{:S(2)}) collective-permute-start(bf16[72,128]{1,0:T(8,128)(2,1)S(1)} %get-tuple-element.53), channel_id=1, source_target_pairs={{0,128},{64,192},{128,0},{192,64},{1,129},{65,193},{129,1},{193,65... | collective-permute-start | bytes 55304 | tf_op jit(solution)/shard_map/ppermute | solution.py:460
  40.1 1.2 %collective-permute-start.2 = (bf16[72,128]{1,0:T(8,128)(2,1)S(1)}, bf16[72,128]{1,0:T(8,128)(2,1)S(1)}, u32[]{:S(2)}, u32[]{:S(2)}) collective-permute-start(bf16[72,128]{1,0:T(8,128)(2,1)S(1)} %get-tuple-element.54), channel_id=1, source_target_pairs={{0,64},{64,128},{128,192},{192,0},{1,65},{65,129},{129,193},{193,1... | collective-permute-start | bytes 55304 | tf_op jit(solution)/shard_map/ppermute | solution.py:460
  41.3 2.4 %collective-permute-start.3 = (bf16[72,128]{1,0:T(8,128)(2,1)S(1)}, bf16[72,128]{1,0:T(8,128)(2,1)S(1)}, u32[]{:S(2)}, u32[]{:S(2)}) collective-permute-start(bf16[72,128]{1,0:T(8,128)(2,1)S(1)} %get-tuple-element.55), channel_id=1, source_target_pairs={{0,192},{64,0},{128,64},{192,128},{1,193},{65,1},{129,65},{193,129... | collective-permute-start | bytes 55304 | tf_op jit(solution)/shard_map/ppermute | solution.py:460
  43.6 0.0 collective-permute-done.1.two_ref
  43.6 1.1 %collective-permute-done.2.one_ref = bf16[72,128]{1,0:T(8,128)(2,1)S(1)} collective-permute-done((bf16[72,128]{1,0:T(8,128)(2,1)S(1)}, bf16[72,128]{1,0:T(8,128)(2,1)S(1)}, u32[]{:S(2)}, u32[]{:S(2)}) %collective-permute-start.2) | collective-permute-done | bytes 18464 | tf_op jit(solution)/shard_map/ppermute | solution.py:460
  44.8 0.2 collective-permute-done.3.three_ref
  45.0 0.4 shard_map.89
  45.4 19.3 %all_to_all.10.refs_10_.pair_ref = bf16[32,128,128]{2,1,0:T(8,128)(2,1)S(1)} all-to-all(bf16[32,128,128]{2,1,0:T(8,128)(2,1)S(1)} %shard_map.89), channel_id=1, replica_groups=mesh['zh'=4,'zl'=2,'y'=4,'x'=4,'core'=2] {'zl','y','x'}, dimensions={0} | all-to-all | bytes 2097152 | tf_op jit(solution)/shard_map/all_to_all | solution.py:466
  64.7 0.2 shard_map.91
  64.9 4.3 %collective-permute-start.4 = (bf16[16,256,128]{2,1,0:T(8,128)(2,1)S(1)}, bf16[16,256,128]{2,1,0:T(8,128)(2,1)S(1)}, u32[]{:S(2)}, u32[]{:S(2)}) collective-permute-start(bf16[16,256,128]{2,1,0:T(8,128)(2,1)S(1)} %shard_map.91), channel_id=1, source_target_pairs={{0,1},{1,0},{2,3},{3,2},{4,5},{5,4},{6,7},{7,6},{8,9},{9,8},{10,11... | collective-permute-start | bytes 3145736 | tf_op jit(solution)/shard_map/ppermute | solution.py:470
  69.2 3.9 %shard_map.90 = (bf16[128,2048]{1,0:T(8,128)(2,1)S(1)}, bf16[128,2048]{1,0:T(8,128)(2,1)S(1)}, bf16[128,2048]{1,0:T(8,128)(2,1)S(1)}, bf16[128,2048]{1,0:T(8,128...) custom-call(s32[1]{0:T(128)} %bitcast.half_ref, ...), custom_call_target="tpu_custom_call" | custom-call | tf_op jit(solution)/shard_map/pallas_call | solution.py:393
  73.1 0.0 collective-permute-done.4.refs_8_
  73.1 2.3 %shard_map.92 = (bf16[128,4096]{1,0:T(8,128)(2,1)}, bf16[128,4096]{1,0:T(8,128)(2,1)}, bf16[128,4096]{1,0:T(8,128)(2,1)}, bf16[128,4096]{1,0:T(8,128)(2,1)}) custom-call(s32[1]{0:T(128)S(6)} %sub.3.half_ref, bf16[32,128]{1,0:T(8,128)(2,1)S(1)} %bitcast.7, bf16[128,2048]{1,0:T(8,128)(2,1)S(1)} %get-tuple-element.57.refs_0_, ...), custom_call_target="tpu_custom_call" | custom-call | tf_op jit(solution)/shard_map/pallas_call | solution.py:393
Async XLA Ops:
  0.6 7.0 %copy-start = (bf16[128,32]{0,1:T(8,128)(2,1)S(1)}, bf16[128,32]{0,1:T(8,128)(2,1)}, u32[]{:S(2)}) copy-start(bf16[128,32]{0,1:T(8,128)(2,1)} %param.9) | copy-start | bytes 24580
  4.3 5.7 %collective-permute-start = (bf16[16,264,128]{2,1,0:T(8,128)(2,1)S(1)}, bf16[16,264,128]{2,1,0:T(8,128)(2,1)S(1)}, u32[]{:S(2)}, u32[]{:S(2)}) collective-permute-start(bf16[16,264,128]{2,1,0:T(8,128)(2,1)S(1)} %get-tuple-element.41), channel_id=1, source_target_pairs={{0,1},{1,0},{2,3},{3,2},{4,5},{5,4},{6,7},{7,6},{8,9},{9,8},{10,11... | collective-permute-start | bytes 3244040 | tf_op jit(solution)/shard_map/ppermute | solution.py:434
  11.1 22.5 %all-to-all-start = ((bf16[32,136,128]{2,1,0:T(8,128)(2,1)}), bf16[32,136,128]{2,1,0:T(8,128)(2,1)S(1)}, u32[]{:S(2)}, u32[]{:S(2)}) async-start(bf16[32,136,128]{2,1,0:T(8,128)(2,1)} %get-tuple-element.42), calls=%async_computation | async-start | bytes 2228224 | tf_op jit(solution)/shard_map/all_to_all | solution.py:442
  34.0 9.7 %collective-permute-start.1 = (bf16[72,128]{1,0:T(8,128)(2,1)S(1)}, bf16[72,128]{1,0:T(8,128)(2,1)S(1)}, u32[]{:S(2)}, u32[]{:S(2)}) collective-permute-start(bf16[72,128]{1,0:T(8,128)(2,1)S(1)} %get-tuple-element.53), channel_id=1, source_target_pairs={{0,128},{64,192},{128,0},{192,64},{1,129},{65,193},{129,1},{193,65... | collective-permute-start | bytes 55304 | tf_op jit(solution)/shard_map/ppermute | solution.py:460
  40.1 4.7 %collective-permute-start.2 = (bf16[72,128]{1,0:T(8,128)(2,1)S(1)}, bf16[72,128]{1,0:T(8,128)(2,1)S(1)}, u32[]{:S(2)}, u32[]{:S(2)}) collective-permute-start(bf16[72,128]{1,0:T(8,128)(2,1)S(1)} %get-tuple-element.54), channel_id=1, source_target_pairs={{0,64},{64,128},{128,192},{192,0},{1,65},{65,129},{129,193},{193,1... | collective-permute-start | bytes 55304 | tf_op jit(solution)/shard_map/ppermute | solution.py:460
  41.3 3.7 %collective-permute-start.3 = (bf16[72,128]{1,0:T(8,128)(2,1)S(1)}, bf16[72,128]{1,0:T(8,128)(2,1)S(1)}, u32[]{:S(2)}, u32[]{:S(2)}) collective-permute-start(bf16[72,128]{1,0:T(8,128)(2,1)S(1)} %get-tuple-element.55), channel_id=1, source_target_pairs={{0,192},{64,0},{128,64},{192,128},{1,193},{65,1},{129,65},{193,129... | collective-permute-start | bytes 55304 | tf_op jit(solution)/shard_map/ppermute | solution.py:460
  64.9 8.2 %collective-permute-start.4 = (bf16[16,256,128]{2,1,0:T(8,128)(2,1)S(1)}, bf16[16,256,128]{2,1,0:T(8,128)(2,1)S(1)}, u32[]{:S(2)}, u32[]{:S(2)}) collective-permute-start(bf16[16,256,128]{2,1,0:T(8,128)(2,1)S(1)} %shard_map.91), channel_id=1, source_target_pairs={{0,1},{1,0},{2,3},{3,2},{4,5},{5,4},{6,7},{7,6},{8,9},{9,8},{10,11... | collective-permute-start | bytes 3145736 | tf_op jit(solution)/shard_map/ppermute | solution.py:470
